TPU v7x, 32 devices: a whole 2x2x4 slice. The times are simulated.
32 devices in a mesh: cam: 4 (over y, core), tile: 8 (over z, x).
Axes of the slice: x: 2, y: 2, z: 4, core: 2. Of those that a mesh axis runs over, the one named last changes fastest.
Arguments:
- tokens: bfloat16 [5632, 1024], P(('cam', 'tile')), may hold values from -16 to 16
- ln_gain: float32 [1024], replicated, may hold values from 0.25 to 1.75
- gate_weight: bfloat16 [1024, 2730], P(('cam', 'tile')), may hold values from -0.1875 to 0.1875
- up_weight: bfloat16 [1024, 2730], P(('cam', 'tile')), may hold values from -0.1875 to 0.1875
- down_weight: bfloat16 [2730, 1024], P(None, ('cam', 'tile')), may hold values from -0.109375 to 0.109375
- head_gain: float32 [1024], replicated, may hold values from 0.25 to 1.75
- depth_weight: bfloat16 [1024, 64], replicated, may hold values from -24 to 24
- context_weight: bfloat16 [1024, 128], replicated, may hold values from -3 to 3
- slot_point: int32 [32, 8, 2503], P(('cam', 'tile')), may hold values from 0 to 11263, as said below
- slot_cell: int32 [32, 8, 2503], P(('cam', 'tile')), may hold values from 0 to 2047
- slot_count: int32 [32, 8], P(('cam', 'tile')), may hold values from 312 to 2503
- conv1_weight: bfloat16 [3, 3, 128, 128], replicated, may hold values from -0.1875 to 0.1875
- conv1_bias: float32 [128], replicated, may hold values from -1.5 to 1.5
- conv2_weight: bfloat16 [3, 3, 128, 128], replicated, may hold values from -0.1875 to 0.1875
- conv2_bias: float32 [128], replicated, may hold values from -1.5 to 1.5
Outputs:
- bev_out: bfloat16 [8, 32, 256, 128], P('cam', 'tile')
Inputs may be any that keep to these rules, and one draw needn't show every extreme that they name: slot_point[s, d, k] is a point of source s; the live slots (k < slot_count[s, d]) of one source name distinct points.
All inputs are finite; a program needn't handle non-finite values.
Results may differ from a plain program's by a relative error of at most 0.013.
The roundings to bfloat16 on the way count: a program that leaves them out, or rounds other values in their place, can miss the bound.
Values may be sent and summed in bfloat16 or wider, within the bound.
A program may use at most 64 MiB of HBM per device.

v0:
```python
import jax
import jax.numpy as jnp
from jax import lax
from jax.experimental import pallas as pl
from jax.experimental.pallas import tpu as pltpu
from jax.sharding import PartitionSpec as P

ROWS_DEV = 4
GRID_W = 256
SCN = 2


def extended_2(value, sides, width):
    for axis, dim in sides:
        size, length = (lax.axis_size(axis), value.shape[dim])
        up = [(i, (i + 1) % size) for i in range(size - 1)]
        down = [(j, i) for i, j in up]
        last = lax.slice_in_dim(value, length - width, length, axis=dim)
        leading = lax.slice_in_dim(value, 0, width, axis=dim)
        before = lax.ppermute(last, axis, up)
        after = lax.ppermute(leading, axis, down)
        value = jnp.concatenate([before, value, after], axis=dim)
    return value


def layer_norm(values, gain):
    center = values - jnp.mean(values, axis=-1, keepdims=True)
    spread = jnp.mean(center * center, axis=-1, keepdims=True)
    return center * lax.rsqrt(spread + 1e-06) * gain


def conv_rows(extended, weight):
    scenes = extended.shape[0]
    out_rows = extended.shape[1] - 2
    columns = extended.shape[2]
    padded = jnp.pad(extended, ((0, 0), (0, 0), (1, 1), (0, 0)))
    total = jnp.zeros((scenes * out_rows * columns, weight.shape[3]), jnp.float32)
    for row_shift in range(3):
        for col_shift in range(3):
            window = padded[:, row_shift : row_shift + out_rows, col_shift : col_shift + columns, :]
            window = window.reshape(-1, weight.shape[2])
            total = total + jnp.dot(
                window, weight[row_shift, col_shift], preferred_element_type=jnp.float32
            )
    return total.reshape(scenes, out_rows, columns, weight.shape[3])


CHUNK = 512


def splat_kernel(rows_ref, table_ref, out_ref, held, send_sem, recv_sem):
    tiles, _, slots = rows_ref.shape
    tokens = table_ref.shape[1]
    half, wide = out_ref.shape
    channels = wide // 2
    bins = table_ref.shape[0] - channels
    chunks = slots // CHUNK
    me = lax.axis_index("tile")

    def table_copy(k):
        return pltpu.make_async_remote_copy(
            src_ref=table_ref,
            dst_ref=held.at[k],
            send_sem=send_sem.at[k],
            recv_sem=recv_sem.at[k],
            device_id={"tile": lax.rem(me - k + tiles, tiles)},
            device_id_type=pl.DeviceIdType.MESH,
        )

    barrier = pltpu.get_barrier_semaphore()

    def greet(k, carry):
        other = lax.rem(me + k, tiles)
        pl.semaphore_signal(
            barrier, inc=1, device_id={"tile": other}, device_id_type=pl.DeviceIdType.MESH
        )
        return carry

    def send(k, carry):
        table_copy(k).start()
        return carry

    def finish(k, carry):
        table_copy(k).wait_send()
        return carry

    lax.fori_loop(1, tiles, greet, 0)
    pl.semaphore_wait(barrier, tiles - 1)
    lax.fori_loop(1, tiles, send, 0)
    out_ref[...] = jnp.zeros_like(out_ref)
    held[0] = table_ref[...]

    def one_source(k, carry):
        @pl.when(k > 0)
        def _():
            table_copy(k).wait_recv()

        source = lax.rem(me + k, tiles)

        def step(i, inner):
            start = pl.multiple_of(i * CHUNK, CHUNK)
            rows = rows_ref[source, :, pl.ds(start, CHUNK)]
            token, depth_bin, cell = rows[0:1], rows[1:2], rows[2:3]
            token_ids = lax.broadcasted_iota(jnp.int32, (tokens, CHUNK), 0)
            pick = jnp.where(token_ids == token, 1.0, 0.0).astype(jnp.bfloat16)
            got = jnp.dot(held[k], pick, preferred_element_type=jnp.float32)
            bin_ids = lax.broadcasted_iota(jnp.int32, (bins, CHUNK), 0)
            weight = jnp.sum(
                jnp.where(bin_ids == depth_bin, got[:bins], 0.0), axis=0, keepdims=True
            )
            upper = cell >= half
            low = jnp.where(upper, 0.0, weight) * got[bins:]
            high = jnp.where(upper, weight, 0.0) * got[bins:]
            lifted = jnp.concatenate([low, high], axis=0).astype(jnp.bfloat16)
            local = jnp.where(upper, cell - half, cell)
            cell_ids = lax.broadcasted_iota(jnp.int32, (half, CHUNK), 0)
            place = jnp.where(cell_ids == local, 1.0, 0.0).astype(jnp.bfloat16)
            out_ref[...] += lax.dot_general(
                place, lifted, (((1,), (1,)), ((), ())), preferred_element_type=jnp.float32
            )
            return inner

        return lax.fori_loop(0, chunks, step, carry)

    lax.fori_loop(0, tiles, one_source, 0)
    lax.fori_loop(1, tiles, finish, 0)


def splat_cells(rows, table, cell_count, channels):
    half = cell_count // 2
    tiles = rows.shape[0]
    out = pl.pallas_call(
        splat_kernel,
        out_shape=jax.ShapeDtypeStruct((half, 2 * channels), jnp.float32),
        in_specs=[pl.BlockSpec(memory_space=pltpu.VMEM)] * 2,
        out_specs=pl.BlockSpec(memory_space=pltpu.VMEM),
        scratch_shapes=[
            pltpu.VMEM((tiles, *table.shape), table.dtype),
            pltpu.SemaphoreType.DMA((tiles,)),
            pltpu.SemaphoreType.DMA((tiles,)),
        ],
        compiler_params=pltpu.CompilerParams(
            collective_id=0, has_side_effects=True, vmem_limit_bytes=48 * 1024 * 1024
        ),
        cost_estimate=pl.CostEstimate(
            flops=2 * cell_count * channels * tiles * rows.shape[2],
            bytes_accessed=4 * cell_count * channels,
            transcendentals=0,
        ),
    )(rows, table)
    return jnp.concatenate([out[:, :channels], out[:, channels:]], axis=0)


def slot_rows(slot_point, slot_cell, slot_count, points, bins_count):
    tiles, slots = slot_point.shape[1:]
    live = jnp.arange(slots, dtype=jnp.int32)[None, :] < slot_count.reshape(tiles, 1)
    packed = jnp.where(live, slot_point.reshape(tiles, slots), points) * 65536
    packed = packed + slot_cell.reshape(tiles, slots)
    got = lax.all_to_all(packed, "tile", split_axis=0, concat_axis=0, tiled=True)
    got = jnp.pad(got, ((0, 0), (0, -slots % CHUNK)), constant_values=points * 65536)
    point = got // 65536
    zero = jnp.zeros_like(got)
    parts = [point // bins_count, point % bins_count, got % 65536]
    return jnp.stack(parts + [zero] * 5, axis=1)


def on_device(
    tokens,
    ln_gain,
    gate_weight,
    up_weight,
    down_weight,
    head_gain,
    depth_weight,
    context_weight,
    slot_point,
    slot_cell,
    slot_count,
    conv1_weight,
    conv1_bias,
    conv2_weight,
    conv2_bias,
):
    tiles = lax.axis_size("tile")
    token_count = tokens.shape[0]
    bins_count = depth_weight.shape[1]
    rows = slot_rows(slot_point, slot_cell, slot_count, token_count * bins_count, bins_count)
    inputs = tokens.astype(jnp.float32)
    normed = layer_norm(inputs, ln_gain).astype(jnp.bfloat16)
    gate_whole, up_whole = (
        lax.all_gather(gate_weight, ("cam", "tile"), axis=0, tiled=True),
        lax.all_gather(up_weight, ("cam", "tile"), axis=0, tiled=True),
    )
    gate_full = jnp.dot(normed, gate_whole, preferred_element_type=jnp.float32)
    up_full = jnp.dot(normed, up_whole, preferred_element_type=jnp.float32)
    hidden = (jax.nn.silu(gate_full) * up_full).astype(jnp.bfloat16)
    down_whole = lax.all_gather(down_weight.T, ("cam", "tile"), axis=0, tiled=True)
    branch_out = lax.dot_general(
        hidden, down_whole, (((1,), (1,)), ((), ())), preferred_element_type=jnp.float32
    )
    updated = inputs + branch_out
    head_input = layer_norm(updated, head_gain).astype(jnp.bfloat16)
    contract = (((0,), (1,)), ((), ()))
    logits = lax.dot_general(
        depth_weight, head_input, contract, preferred_element_type=jnp.float32
    )
    context = lax.dot_general(
        context_weight, head_input, contract, preferred_element_type=jnp.float32
    )
    depth = jax.nn.softmax(logits, axis=0)
    channels = context.shape[0]
    table = jnp.concatenate([depth, context], axis=0).astype(jnp.bfloat16)
    cell_count = SCN * ROWS_DEV * GRID_W
    splat = splat_cells(rows, table, cell_count, channels)
    bev = splat.astype(jnp.bfloat16).reshape(SCN, ROWS_DEV, GRID_W, channels)
    extended = extended_2(bev, (("tile", 1),), 2)
    middle_wide = jnp.maximum(conv_rows(extended, conv1_weight) + conv1_bias, 0.0)
    global_rows = lax.axis_index("tile") * ROWS_DEV - 1 + jnp.arange(ROWS_DEV + 2, dtype=jnp.int32)
    inside = (global_rows >= 0) & (global_rows < tiles * ROWS_DEV)
    middle_ext = jnp.where(inside[None, :, None, None], middle_wide, 0.0).astype(jnp.bfloat16)
    result = bev.astype(jnp.float32) + conv_rows(middle_ext, conv2_weight) + conv2_bias
    return result.astype(jnp.bfloat16)


def solution(mesh):
    return jax.shard_map(
        on_device,
        mesh=mesh,
        in_specs=(
            P(("cam", "tile"), None),
            P(),
            P(("cam", "tile"), None),
            P(("cam", "tile"), None),
            P(None, ("cam", "tile")),
            P(),
            P(),
            P(),
            P(("cam", "tile"), None, None),
            P(("cam", "tile"), None, None),
            P(("cam", "tile"), None),
            P(),
            P(),
            P(),
            P(),
        ),
        out_specs=P("cam", "tile", None, None),
        check_vma=False,
    )
```

profile of v0, /device:TPU:0, one launch (start us, length us, event | category | flops | bytes accessed | tf_op | source)
XLA Modules:
  0.0 294.8 jit_solution(15668558754558991822)
XLA Ops:
  6.5 0.7 all-gather.4.cloned.1.call-update
  7.3 0.7 all-gather.6.cloned.1.call-update
  8.1 0.7 all-gather.8.cloned.1.call-update
  8.7 1.7 fusion.24
  10.5 7.3 %all-to-all-start = ((s32[8,1,2503]{2,1,0:T(1,128)}), s32[8,1,2503]{2,1,0:T(1,128)S(1)}, u32[]{:S(2)}, u32[]{:S(2)}) async-start(s32[8,1,2503]{2,1,0:T(1,128)} %fusion.24), calls=%async_computation | async-start | bytes 163840 | tf_op jit(solution)/shard_map/all_to_all | solution.py:159
  17.8 1.1 convert_reduce_fusion
  18.9 1.3 fusion.5
  20.2 4.7 %all-to-all-done = s32[8,1,2503]{2,1,0:T(1,128)S(1)} async-done(((s32[8,1,2503]{2,1,0:T(1,128)}), s32[8,1,2503]{2,1,0:T(1,128)S(1)}, u32[]{:S(2)}, u32[]{:S(2)}) %all-to-all-start) | async-done | bytes 80128 | tf_op jit(solution)/shard_map/all_to_all | solution.py:159
  25.4 1.1 stack.19.rows_ref
  26.5 53.8 %all-gather.4.cloned.1.call-done = bf16[1024,2730]{1,0:T(8,128)(2,1)} async-done(((bf16[32,2730]{1,0:T(8,128)(2,1)}), bf16[1024,2730]{1,0:T(8,128)(2,1)}) %all-gather.4.cloned.1.call-update) | async-done | bytes 5591056 | tf_op jit(solution)/shard_map/all_gather | solution.py:191
  80.3 5.2 %fusion.10 = f32[176,2730]{1,0:T(8,128)} fusion(bf16[1024,2730]{1,0:T(8,128)(2,1)} %all-gather.4.cloned.1.call-done, bf16[176,1024]{1,0:T(8,128)(2,1)S(1)} %copy-done.1, f32[1024]{0:T(1024)S(1)} %copy-done.8, f32[176]{0:T(256)S(1)} %add_rsqrt_fusion.1, f32[176]{0:T(256)S(1)} %broadcast_multiply_fusion.1), kind=kOutput, calls=%fused_computation.42 | convolution fusion | flops 984924160 | bytes 7878912 | tf_op jit(solution)/shard_map/dot_general | solution.py:194
  85.6 63.7 %all-gather.6.cloned.1.call-done = bf16[1024,2730]{1,0:T(8,128)(2,1)} async-done(((bf16[32,2730]{1,0:T(8,128)(2,1)}), bf16[1024,2730]{1,0:T(8,128)(2,1)}) %all-gather.6.cloned.1.call-update) | async-done | bytes 5591056 | tf_op jit(solution)/shard_map/all_gather | solution.py:192
  149.2 68.9 %all-gather.8.cloned.1.call-done = bf16[1024,2730]{1,0:T(8,128)(2,1)} async-done(((bf16[32,2730]{1,0:T(8,128)(2,1)}), bf16[1024,2730]{1,0:T(8,128)(2,1)}) %all-gather.8.cloned.1.call-update) | async-done | bytes 5591056 | tf_op jit(solution)/shard_map/all_gather | solution.py:197
  218.2 7.9 %fusion.73 = (f32[176]{0:T(256)S(1)}, f32[176,1024]{1,0:T(8,128)S(1)}) fusion(bf16[1024,2730]{1,0:T(8,128)(2,1)} %all-gather.8.cloned.1.call-done, bf16[1024,2730]{1,0:T(8,128)(2,1)} %all-gather.6.cloned.1.call-done, f32[176,2730]{1,0:T(8,128)} %fusion.10, bf16[176,1024]{1,0:T(8,128)(2,1)S(1)} %copy-done.1, f32[1024]{0:T(1024)S(1)} %copy-done.8, ...), kind=kOutput, calls=%fused_computation.130 | convolution fusion | flops 1972370688 | bytes 14191552 | tf_op jit(solution)/shard_map/dot_general | solution.py:198
  226.5 0.5 copy-done.4
  227.7 34.9 %shard_map.145 = f32[1024,256]{1,0:T(8,128)S(1)} custom-call(s32[8,8,2560]{2,1,0:T(8,128)S(1)} %stack.19.rows_ref, bf16[192,176]{1,0:T(8,128)(2,1)S(1)} %pad_maximum_fusion.4.table_ref), custom_call_target="tpu_custom_call" | custom-call | flops 10737418240 | bytes 1048576 | tf_op jit(solution)/shard_map/pallas_call | solution.py:132
  262.8 5.3 %collective-permute-start = (bf16[2,2,256,128]{3,2,1,0:T(8,128)(2,1)S(1)}, bf16[2,2,256,128]{3,2,1,0:T(8,128)(2,1)S(1)}, u32[]{:S(2)}, u32[]{:S(2)}) collective-permute-start(bf16[2,2,256,128]{3,2,1,0:T(8,128)(2,1)S(1)} %get-tuple-element.23), channel_id=1, source_target_pairs={{0,1},{1,2},{2,3},{3,4},{4,5},{5,6},{6,7},{8,9},{9,10},{10,11},{11... | collective-permute-start | bytes 786440 | tf_op jit(solution)/shard_map/ppermute | solution.py:20
  268.1 1.5 collective-permute-start.1
  269.6 8.5 %collective-permute-done = bf16[2,2,256,128]{3,2,1,0:T(8,128)(2,1)S(1)} collective-permute-done((bf16[2,2,256,128]{3,2,1,0:T(8,128)(2,1)S(1)}, bf16[2,2,256,128]{3,2,1,0:T(8,128)(2,1)S(1)}, u32[]{:S(2)}, u32[]{:S(2)}) %collective-permute-start) | collective-permute-done | bytes 262176 | tf_op jit(solution)/shard_map/ppermute | solution.py:20
  278.2 1.3 pad_slice_fusion.1
  282.5 0.4 fusion.1
  283.4 1.0 pad_slice_fusion.6
  287.0 0.4 copy-done.6
  287.3 0.9 add_convert_fusion
  (64 shorter events, 7.9 us)
Async XLA Ops:
  6.5 220.8 %copy-start = (bf16[1024,128]{1,0:T(8,128)(2,1)S(1)}, bf16[1024,128]{1,0:T(8,128)(2,1)}, u32[]{:S(2)}) copy-start(bf16[1024,128]{1,0:T(8,128)(2,1)} %param.22) | copy-start | bytes 786436
  6.5 73.8 %all-gather.4.cloned.1.call-start = ((), (), s32[]{:S(2)}) async-start(), calls=%async_computation.1 | async-start | bytes 5947392 | tf_op jit(solution)/shard_map/all_gather | solution.py:191
  7.3 142.0 %all-gather.6.cloned.1.call-start = ((), (), s32[]{:S(2)}) async-start(), calls=%async_computation.2 | async-start | bytes 5947392 | tf_op jit(solution)/shard_map/all_gather | solution.py:192
  8.0 210.2 %all-gather.8.cloned.1.call-start = ((), (), s32[]{:S(2)}) async-start(), calls=%async_computation.3 | async-start | bytes 5947392 | tf_op jit(solution)/shard_map/all_gather | solution.py:197
  10.5 14.4 %all-to-all-start = ((s32[8,1,2503]{2,1,0:T(1,128)}), s32[8,1,2503]{2,1,0:T(1,128)S(1)}, u32[]{:S(2)}, u32[]{:S(2)}) async-start(s32[8,1,2503]{2,1,0:T(1,128)} %fusion.24), calls=%async_computation | async-start | bytes 163840 | tf_op jit(solution)/shard_map/all_to_all | solution.py:159
  18.9 61.5 %copy-start.1 = (bf16[176,1024]{1,0:T(8,128)(2,1)S(1)}, bf16[176,1024]{1,0:T(8,128)(2,1)}, u32[]{:S(2)}) copy-start(bf16[176,1024]{1,0:T(8,128)(2,1)} %param.15) | copy-start | bytes 1081348
  18.9 61.5 %copy-start.8 = (f32[1024]{0:T(1024)S(1)}, f32[1024]{0:T(1024)}, u32[]{:S(2)}) copy-start(f32[1024]{0:T(1024)} %param.16) | copy-start | bytes 12292
  85.6 140.7 %copy-start.5 = (f32[1024]{0:T(1024)S(1)}, f32[1024]{0:T(1024)}, u32[]{:S(2)}) copy-start(f32[1024]{0:T(1024)} %param.20) | copy-start | bytes 12292
  226.0 0.9 copy-start.4
  262.8 15.3 %collective-permute-start = (bf16[2,2,256,128]{3,2,1,0:T(8,128)(2,1)S(1)}, bf16[2,2,256,128]{3,2,1,0:T(8,128)(2,1)S(1)}, u32[]{:S(2)}, u32[]{:S(2)}) collective-permute-start(bf16[2,2,256,128]{3,2,1,0:T(8,128)(2,1)S(1)} %get-tuple-element.23), channel_id=1, source_target_pairs={{0,1},{1,2},{2,3},{3,4},{4,5},{5,6},{6,7},{8,9},{9,10},{10,11},{11... | collective-permute-start | bytes 786440 | tf_op jit(solution)/shard_map/ppermute | solution.py:20
  268.1 10.0 %collective-permute-start.1 = (bf16[2,2,256,128]{3,2,1,0:T(8,128)(2,1)S(1)}, bf16[2,2,256,128]{3,2,1,0:T(8,128)(2,1)S(1)}, u32[]{:S(2)}, u32[]{:S(2)}) collective-permute-start(bf16[2,2,256,128]{3,2,1,0:T(8,128)(2,1)S(1)} %get-tuple-element.24), channel_id=1, source_target_pairs={{1,0},{2,1},{3,2},{4,3},{5,4},{6,5},{7,6},{9,8},{10,9},{11,10},{12... | collective-permute-start | bytes 786440 | tf_op jit(solution)/shard_map/ppermute | solution.py:21
  278.2 1.3 copy-start.2
  282.5 0.7 copy-start.7
  283.4 1.0 copy-start.3
  286.7 0.7 copy-start.6
Sparse Core Ops, SparseCore 0:
  10.2 70.0 all-gather.3
  83.2 65.9 all-gather.5
  152.2 65.9 all-gather.7
where the time goes:
time: 295 us
  waiting for transfers between devices  202 us (68%)
  Pallas kernels  34.9 us (12%)
  matrix products  19.3 us (7%)
  starting transfers between devices  14.1 us (5%)
  between operations  13.5 us (5%)
  other arithmetic  6.3 us (2%)
  local copies, waits for them, and re-layouts  5 us (2%)
    all_gather x1, waiting for transfers between devices, on_device(): lax.all_gather(down_weight.T, ('cam', 'tile'), axis=0, tiled=True)  68.9 us
    all_gather x1, waiting for transfers between devices, on_device(): lax.all_gather(up_weight, ('cam', 'tile'), axis=0, tiled=True)  63.7 us
    all_gather x1, waiting for transfers between devices, on_device(): lax.all_gather(gate_weight, ('cam', 'tile'), axis=0, tiled=True)  53.8 us
    pallas_call x1, Pallas kernels, splat_cells(): pl.pallas_call(splat_kernel, out_shape=jax.ShapeDtypeStruct((half, 2 * ch...  34.9 us
    ppermute x1, waiting for transfers between devices, extended_2(): before = lax.ppermute(last, axis, up)  8.49 us
    dot_general x1, matrix products, on_device(): lax.dot_general(hidden, down_whole, (((1,), (1,)), ((), ())), preferred_e...  7.89 us
    all_to_all x1, starting transfers between devices, slot_rows(): lax.all_to_all(packed, 'tile', split_axis=0, concat_axis=0, tiled=True)  7.28 us
  transfers between devices with their start and end apart: 6, of which 5 were waited for; matrix products, arithmetic and copies ran while one was open for 4% of the time, Pallas kernels for 0%

commit v1 on v0

v1 whole, which is shorter than its diff:
```python
import functools

import jax
import jax.numpy as jnp
from jax import lax
from jax.experimental import pallas as pl
from jax.experimental.pallas import tpu as pltpu
from jax.sharding import PartitionSpec as P

ROWS_DEV = 4
GRID_W = 256
SCN = 2
CHUNK = 512
LANES = 128
MESH = pl.DeviceIdType.MESH


def layer_norm(values, gain):
    center = values - jnp.mean(values, axis=-1, keepdims=True)
    spread = jnp.mean(center * center, axis=-1, keepdims=True)
    return center * lax.rsqrt(spread + 1e-06) * gain


def remote(src, dst, send, recv, cam, tile):
    return pltpu.make_async_remote_copy(
        src_ref=src,
        dst_ref=dst,
        send_sem=send,
        recv_sem=recv,
        device_id={"cam": cam, "tile": tile},
        device_id_type=MESH,
    )


def soft_table(scores, bins):
    logits = scores[:bins]
    top = jnp.max(logits, axis=0, keepdims=True)
    raised = jnp.exp(logits - top)
    depth = raised / jnp.sum(raised, axis=0, keepdims=True)
    return jnp.concatenate([depth, scores[bins:]], axis=0).astype(jnp.bfloat16)


class Exchange:
    def __init__(self, tiles, own, whole, recv, up, down, side, core, pair):
        self.cam, self.tile = lax.axis_index("cam"), lax.axis_index("tile")
        self.tiles, self.depth = tiles, tiles // 2
        self.y, self.c = self.cam // 2, lax.rem(self.cam, 2)
        self.z, self.x = self.tile // 2, lax.rem(self.tile, 2)
        self.own, self.whole, self.recv = own, whole, recv
        self.up, self.down, self.side, self.core, self.pair = up, down, side, core, pair
        self.rows = own.shape[2]
        self.span = ((0, 2), (2, 1))

    def shard(self, y, c, z, x):
        return (2 * y + c) * self.tiles + 2 * z + x

    def block(self, kind, shard):
        first, count = self.span[kind]
        rows = pl.ds(pl.multiple_of(shard * self.rows, self.rows), self.rows)
        return self.whole.at[pl.ds(first, count), rows, :]

    def mine(self, kind, half):
        first, count = self.span[kind]
        return self.own.at[half, pl.ds(first, count)]

    def to(self, route, kind, y, z, x):
        shard = self.shard(y, self.c, z, x)
        block = self.block(kind, shard)
        q = 2 * z + x
        got = self.recv.at[kind, shard]
        if route == "up":
            return remote(block, block, self.up.at[kind, q], got, self.cam, self.tile + 2)
        if route == "down":
            return remote(block, block, self.down.at[kind, q], got, self.cam, self.tile - 2)
        if route == "side":
            other = 2 * (1 - self.y) + self.c
            return remote(block, block, self.side.at[kind, q], got, other, self.tile)
        other = 2 * self.y + 1 - self.c
        return remote(block, block, self.core.at[kind, y, q], got, other, self.tile)

    def across(self, kind):
        shard = self.shard(self.y, self.c, self.z, self.x)
        return remote(
            self.mine(kind, 1 - self.x),
            self.block(kind, shard),
            self.pair.at[kind],
            self.recv.at[kind, shard],
            self.cam,
            self.tile + 1 - 2 * self.x,
        )

    def wait(self, kind, y, c, z, x):
        shard = self.shard(y, c, z, x)
        block = self.block(kind, shard)
        remote(
            block, block, self.pair.at[kind], self.recv.at[kind, shard], self.cam, self.tile
        ).wait_recv()

    def spread(self, kind, x):
        def go_up():
            self.to("up", kind, self.y, self.z, x).start()

        def go_down():
            self.to("down", kind, self.y, self.z, x).start()

        pl.when(self.z + 1 < self.depth)(go_up)
        pl.when(self.z > 0)(go_down)
        self.to("side", kind, self.y, self.z, x).start()
        self.to("core", kind, self.y, self.z, x).start()

    def relay(self, kind, d):
        for step in range(2):
            x = self.x if step == 0 else 1 - self.x

            def below():
                z = self.z - d
                self.wait(kind, self.y, self.c, z, x)

                def go_up():
                    self.to("up", kind, self.y, z, x).start()

                pl.when(self.z + 1 < self.depth)(go_up)
                self.to("side", kind, self.y, z, x).start()
                self.to("core", kind, self.y, z, x).start()

            def above():
                z = self.z + d
                self.wait(kind, self.y, self.c, z, x)

                def go_down():
                    self.to("down", kind, self.y, z, x).start()

                pl.when(self.z > 0)(go_down)
                self.to("side", kind, self.y, z, x).start()
                self.to("core", kind, self.y, z, x).start()

            pl.when(self.z - d >= 0)(below)
            pl.when(self.z + d < self.depth)(above)

    def crossed(self, kind, d):
        y = 1 - self.y

        def take(z):
            for step in range(2):
                x = self.x if step == 0 else 1 - self.x
                self.wait(kind, y, self.c, z, x)
                self.to("core", kind, y, z, x).start()

        if d == 0:
            take(self.z)
            return
        pl.when(self.z - d >= 0)(lambda: take(self.z - d))
        pl.when(self.z + d < self.depth)(lambda: take(self.z + d))

    def beside(self, kind, y):
        for z in range(self.depth):
            for x in range(2):
                self.wait(kind, y, 1 - self.c, z, x)

    def finish(self):
        for kind in range(2):
            self.across(kind).wait_send()
            for q in range(self.tiles):
                z, x = q // 2, q % 2

                def up():
                    self.to("up", kind, self.y, z, x).wait_send()

                def down():
                    self.to("down", kind, self.y, z, x).wait_send()

                pl.when((self.z >= z) & (self.z + 1 < self.depth))(up)
                pl.when((self.z <= z) & (self.z > 0))(down)
                self.to("side", kind, self.y, z, x).wait_send()
                for y in range(2):
                    self.to("core", kind, y, z, x).wait_send()


def feed_forward(ex, tokens, gain, guest, normed, gate, up, hidden, kept, sent, came, sems):
    local, tok_send, tok_recv, part_send, part_recv = sems
    count = tokens.shape[0]
    mate = ex.tile + 1 - 2 * ex.x
    token_copy = remote(tokens, guest, tok_send, tok_recv, ex.cam, mate)
    me = ex.shard(ex.y, ex.c, ex.z, ex.x)
    copies = [
        pltpu.make_async_copy(ex.mine(kind, ex.x), ex.block(kind, me), local.at[kind])
        for kind in range(2)
    ]
    ex.across(0).start()
    for copy in copies:
        copy.start()
    copies[0].wait()
    ex.spread(0, ex.x)
    token_copy.start()
    ex.across(1).start()
    normed[:count] = layer_norm(tokens[...].astype(jnp.float32), gain[...]).astype(jnp.bfloat16)
    ex.wait(0, ex.y, ex.c, ex.z, 1 - ex.x)
    ex.spread(0, 1 - ex.x)
    ex.relay(0, 1)
    copies[1].wait()
    token_copy.wait_recv()
    normed[count:] = layer_norm(guest[...].astype(jnp.float32), gain[...]).astype(jnp.bfloat16)
    ex.crossed(0, 0)
    for d in range(2, ex.depth):
        ex.relay(0, d)
        ex.crossed(0, d - 1)
    ex.spread(1, ex.x)
    ex.wait(1, ex.y, ex.c, ex.z, 1 - ex.x)
    ex.spread(1, 1 - ex.x)
    wide = ex.rows * ex.tiles

    def project(cam, first):
        rows = pl.ds(pl.multiple_of(cam * wide, wide), wide)
        for which, total in ((0, gate), (1, up)):
            got = jnp.dot(
                normed[:, rows], ex.whole[which, rows, :], preferred_element_type=jnp.float32
            )
            if first:
                total[...] = got
            else:
                total[...] += got

    def columns(piece):
        rows = pl.ds(pl.multiple_of(piece * LANES, LANES), LANES)
        got = lax.dot_general(
            hidden[...],
            ex.whole[2, rows, :],
            (((1,), (1,)), ((), ())),
            preferred_element_type=jnp.float32,
        )
        kept[piece] = got[:count]
        sent[piece] = got[count:]
        part(piece).start()

    def part(piece):
        return remote(
            sent.at[piece], came.at[piece], part_send.at[piece], part_recv.at[piece], ex.cam, mate
        )

    project(2 * ex.y + ex.c, True)
    ex.relay(1, 1)
    ex.beside(0, ex.y)
    project(2 * ex.y + 1 - ex.c, False)
    ex.crossed(0, ex.depth - 1)
    for d in range(2, ex.depth):
        ex.relay(1, d)
    project(2 * (1 - ex.y) + ex.c, False)
    ex.beside(0, 1 - ex.y)
    project(2 * (1 - ex.y) + 1 - ex.c, False)
    value = gate[...]
    hidden[...] = (value / (1.0 + jnp.exp(-value)) * up[...]).astype(jnp.bfloat16)
    pieces = wide // LANES
    for half in range(pieces):
        columns((2 * ex.y + ex.c) * pieces + half)
    for d in range(ex.depth):
        ex.crossed(1, d)
    ex.beside(1, ex.y)
    for half in range(pieces):
        columns((2 * ex.y + 1 - ex.c) * pieces + half)
    for half in range(pieces):
        columns((2 * (1 - ex.y) + ex.c) * pieces + half)
    ex.beside(1, 1 - ex.y)
    for half in range(pieces):
        columns((2 * (1 - ex.y) + 1 - ex.c) * pieces + half)
    for piece in range(kept.shape[0]):
        part(piece).wait_recv()
    blocks = [kept[piece] + came[piece] for piece in range(kept.shape[0])]
    updated = tokens[...].astype(jnp.float32) + jnp.concatenate(blocks, axis=1)

    def finish():
        token_copy.wait_send()
        for piece in range(kept.shape[0]):
            part(piece).wait_send()
        ex.finish()

    return updated, finish


def splat(table, held, slots, total, tiles, me, bins, arrived):
    half, wide = total.shape
    tokens = table.shape[1]
    chunks = slots.shape[2] // CHUNK
    total[...] = jnp.zeros_like(total)
    held[0] = table[...]

    def one_source(k, carry):
        arrived(k)
        source = lax.rem(me + k, tiles)

        def step(i, inner):
            start = pl.multiple_of(i * CHUNK, CHUNK)
            packed = slots[source, :, pl.ds(start, CHUNK)]
            point, cell = packed // 65536, packed % 65536
            token, depth_bin = point // bins, point % bins
            token_ids = lax.broadcasted_iota(jnp.int32, (tokens, CHUNK), 0)
            pick = jnp.where(token_ids == token, 1.0, 0.0).astype(jnp.bfloat16)
            got = jnp.dot(held[k], pick, preferred_element_type=jnp.float32)
            bin_ids = lax.broadcasted_iota(jnp.int32, (bins, CHUNK), 0)
            weight = jnp.sum(
                jnp.where(bin_ids == depth_bin, got[:bins], 0.0), axis=0, keepdims=True
            )
            upper = cell >= half
            low = jnp.where(upper, 0.0, weight) * got[bins:]
            high = jnp.where(upper, weight, 0.0) * got[bins:]
            lifted = jnp.concatenate([low, high], axis=0).astype(jnp.bfloat16)
            local = jnp.where(upper, cell - half, cell)
            cell_ids = lax.broadcasted_iota(jnp.int32, (half, CHUNK), 0)
            place = jnp.where(cell_ids == local, 1.0, 0.0).astype(jnp.bfloat16)
            total[...] += lax.dot_general(
                place, lifted, (((1,), (1,)), ((), ())), preferred_element_type=jnp.float32
            )
            return inner

        return lax.fori_loop(0, chunks, step, carry)

    lax.fori_loop(0, tiles, one_source, 0)


def widen(source, index, wide, row):
    value = source[index].astype(jnp.float32)
    columns, channels = value.shape
    places = lax.broadcasted_iota(jnp.int32, (columns, channels), 0)
    left = jnp.where(places == 0, 0.0, pltpu.roll(value, 1, 0))
    right = jnp.where(places == columns - 1, 0.0, pltpu.roll(value, columns - 1, 0))
    wide[row] = jnp.concatenate([left, value, right], axis=1).astype(jnp.bfloat16)


def convolve(wide, row, weight):
    total = None
    for shift in range(3):
        got = jnp.dot(wide[row + shift], weight[shift], preferred_element_type=jnp.float32)
        total = got if total is None else total + got
    return total


def program(fused, tiles, bins, *refs):
    if fused:
        (tokens, gain, own, head_gain, head, slot_in, w1, b1, w2, b2, out) = refs[:11]
        (slots, table, held, total, ext, wide, mid, wide_mid) = refs[11:19]
        (slot_send, slot_recv, table_send, table_recv, halo_send, halo_recv) = refs[19:25]
        (whole, guest, normed, gate, up, hidden, kept, sent, came) = refs[25:34]
        (recv, zup, zdown, side, core, pair) = refs[34:40]
        sems = refs[40:45]
    else:
        (table_in, slot_in, w1, b1, w2, b2, out) = refs[:7]
        (slots, table, held, total, ext, wide, mid, wide_mid) = refs[7:15]
        (slot_send, slot_recv, table_send, table_recv, halo_send, halo_recv) = refs[15:21]
    cam, me = lax.axis_index("cam"), lax.axis_index("tile")
    barrier = pltpu.get_barrier_semaphore()

    def greet(k, carry):
        other = lax.rem(me + k, tiles)
        pl.semaphore_signal(
            barrier, inc=1, device_id={"cam": cam, "tile": other}, device_id_type=MESH
        )
        return carry

    lax.fori_loop(1, tiles, greet, 0)
    extra = 0
    if fused:
        y, c = cam // 2, lax.rem(cam, 2)
        for other in (2 * (1 - y) + c, 2 * y + 1 - c):
            pl.semaphore_signal(
                barrier, inc=1, device_id={"cam": other, "tile": me}, device_id_type=MESH
            )
            extra += 1
    pl.semaphore_wait(barrier, tiles - 1 + extra)

    def slot_copy(k):
        other = lax.rem(me + k, tiles)
        return remote(slot_in.at[other], slots.at[me], slot_send.at[k], slot_recv.at[k], cam, other)

    def slot_wait(k):
        source = lax.rem(me - k + tiles, tiles)
        remote(
            slot_in.at[me], slots.at[source], slot_send.at[k], slot_recv.at[k], cam, me
        ).wait_recv()

    def slot_start(k, carry):
        slot_copy(k).start()
        return carry

    def slot_finish(k, carry):
        slot_wait(k)
        slot_copy(k).wait_send()
        return carry

    lax.fori_loop(1, tiles, slot_start, 0)
    own_slots = pltpu.make_async_copy(slot_in.at[me], slots.at[me], slot_send.at[0])
    own_slots.start()
    if fused:
        ex = Exchange(tiles, own, whole, recv, zup, zdown, side, core, pair)
        updated, finish = feed_forward(
            ex, tokens, gain, guest, normed, gate, up, hidden, kept, sent, came, sems
        )
        head_input = layer_norm(updated, head_gain[...]).astype(jnp.bfloat16)
        scores = lax.dot_general(
            head[...], head_input, (((1,), (1,)), ((), ())), preferred_element_type=jnp.float32
        )
        table[...] = soft_table(scores, bins)
    else:
        table[...] = table_in[...]

    def table_copy(k):
        other = lax.rem(me - k + tiles, tiles)
        return remote(table, held.at[k], table_send.at[k], table_recv.at[k], cam, other)

    def table_start(k, carry):
        table_copy(k).start()
        return carry

    def table_finish(k, carry):
        table_copy(k).wait_send()
        return carry

    lax.fori_loop(1, tiles, table_start, 0)
    own_slots.wait()
    lax.fori_loop(1, tiles, slot_finish, 0)

    def arrived(k):
        pl.when(k > 0)(lambda: table_copy(k).wait_recv())

    splat(table, held, slots, total, tiles, me, bins, arrived)
    channels = total.shape[1] // 2
    per_scene = ROWS_DEV * GRID_W
    for scene in range(SCN):
        for row in range(ROWS_DEV):
            start = scene * per_scene + row * GRID_W
            side_of, first = divmod(start, total.shape[0])
            ext[scene, 2 + row] = total[
                first : first + GRID_W, side_of * channels : (side_of + 1) * channels
            ].astype(jnp.bfloat16)

    def halo(which):
        if which == 0:
            src, dst, other = ext.at[:, 2:4], ext.at[:, ROWS_DEV + 2 : ROWS_DEV + 4], me - 1
        else:
            src, dst, other = ext.at[:, ROWS_DEV : ROWS_DEV + 2], ext.at[:, 0:2], me + 1
        return remote(src, dst, halo_send.at[which], halo_recv.at[which], cam, other)

    blank = jnp.zeros((SCN, 2, GRID_W, channels), jnp.bfloat16)

    def first_tile():
        ext[:, 0:2] = blank

    def last_tile():
        ext[:, ROWS_DEV + 2 : ROWS_DEV + 4] = blank

    has_before, has_after = me > 0, me + 1 < tiles
    pl.when(has_before)(lambda: halo(0).start())
    pl.when(has_after)(lambda: halo(1).start())
    pl.when(me == 0)(first_tile)
    pl.when(me + 1 == tiles)(last_tile)
    rows_ext = ROWS_DEV + 4
    for scene in range(SCN):
        for row in range(2, ROWS_DEV + 2):
            widen(ext, (scene, row), wide, scene * rows_ext + row)
    pl.when(has_before)(lambda: halo(1).wait_recv())
    pl.when(has_after)(lambda: halo(0).wait_recv())
    for scene in range(SCN):
        for row in (0, 1, ROWS_DEV + 2, ROWS_DEV + 3):
            widen(ext, (scene, row), wide, scene * rows_ext + row)
    rows_mid = ROWS_DEV + 2
    for scene in range(SCN):
        for row in range(rows_mid):
            value = jnp.maximum(convolve(wide, scene * rows_ext + row, w1) + b1[...], 0.0)
            if row == 0:
                value = jnp.where(has_before, value, 0.0)
            if row == rows_mid - 1:
                value = jnp.where(has_after, value, 0.0)
            mid[scene, row] = value.astype(jnp.bfloat16)
            widen(mid, (scene, row), wide_mid, scene * rows_mid + row)
    for scene in range(SCN):
        for row in range(ROWS_DEV):
            value = convolve(wide_mid, scene * rows_mid + row, w2) + b2[...]
            value = ext[scene, 2 + row].astype(jnp.float32) + value
            out[scene, row] = value.astype(jnp.bfloat16)
    pl.when(has_before)(lambda: halo(0).wait_send())
    pl.when(has_after)(lambda: halo(1).wait_send())
    lax.fori_loop(1, tiles, table_finish, 0)
    if fused:
        finish()


def run(fused, arrays, slots, weights, sizes):
    tiles, bins, channels, token_count = sizes
    cells = SCN * ROWS_DEV * GRID_W
    dma = pltpu.SemaphoreType.DMA
    bf16, f32 = jnp.bfloat16, jnp.float32
    scratch = [
        pltpu.VMEM(slots.shape, jnp.int32),
        pltpu.VMEM((bins + channels, token_count), bf16),
        pltpu.VMEM((tiles, bins + channels, token_count), bf16),
        pltpu.VMEM((cells // 2, 2 * channels), f32),
        pltpu.VMEM((SCN, ROWS_DEV + 4, GRID_W, channels), bf16),
        pltpu.VMEM((SCN * (ROWS_DEV + 4), GRID_W, 3 * channels), bf16),
        pltpu.VMEM((SCN, ROWS_DEV + 2, GRID_W, channels), bf16),
        pltpu.VMEM((SCN * (ROWS_DEV + 2), GRID_W, 3 * channels), bf16),
        dma((tiles,)),
        dma((tiles,)),
        dma((tiles,)),
        dma((tiles,)),
        dma((2,)),
        dma((2,)),
    ]
    if fused:
        tokens, own = arrays[0], arrays[2]
        count, width = tokens.shape
        cams = lax.axis_size("cam")
        half = own.shape[3]
        pieces = width // LANES
        scratch += [
            pltpu.VMEM((3, width, half), bf16),
            pltpu.VMEM((count, width), bf16),
            pltpu.VMEM((2 * count, width), bf16),
            pltpu.VMEM((2 * count, half), f32),
            pltpu.VMEM((2 * count, half), f32),
            pltpu.VMEM((2 * count, half), bf16),
            pltpu.VMEM((pieces, count, LANES), f32),
            pltpu.VMEM((pieces, count, LANES), f32),
            pltpu.VMEM((pieces, count, LANES), f32),
            dma((2, cams * tiles)),
            dma((2, tiles)),
            dma((2, tiles)),
            dma((2, tiles)),
            dma((2, 2, tiles)),
            dma((2,)),
            dma((2,)),
            dma,
            dma,
            dma((pieces,)),
            dma((pieces,)),
        ]
    operands = [*arrays, slots, *weights]
    return pl.pallas_call(
        functools.partial(program, fused, tiles, bins),
        out_shape=jax.ShapeDtypeStruct((SCN, ROWS_DEV, GRID_W, channels), bf16),
        in_specs=[pl.BlockSpec(memory_space=pltpu.VMEM)] * len(operands),
        out_specs=pl.BlockSpec(memory_space=pltpu.VMEM),
        scratch_shapes=scratch,
        compiler_params=pltpu.CompilerParams(
            collective_id=0, has_side_effects=True, vmem_limit_bytes=60 * 1024 * 1024
        ),
    )(*operands)


def packed_slots(slot_point, slot_cell, slot_count, points):
    tiles, slots = slot_point.shape[1:]
    live = jnp.arange(slots, dtype=jnp.int32)[None, :] < slot_count.reshape(tiles, 1)
    packed = jnp.where(live, slot_point.reshape(tiles, slots), points) * 65536
    packed = packed + slot_cell.reshape(tiles, slots)
    packed = jnp.pad(packed, ((0, 0), (0, -slots % CHUNK)), constant_values=points * 65536)
    return packed.reshape(tiles, 1, -1)


def table_of(tokens, ln_gain, gate_weight, up_weight, down_weight, head_gain, head):
    inputs = tokens.astype(jnp.float32)
    normed = layer_norm(inputs, ln_gain).astype(jnp.bfloat16)
    axes = ("cam", "tile")
    gate_whole = lax.all_gather(gate_weight, axes, axis=0, tiled=True)
    up_whole = lax.all_gather(up_weight, axes, axis=0, tiled=True)
    gate = jnp.dot(normed, gate_whole, preferred_element_type=jnp.float32)
    up = jnp.dot(normed, up_whole, preferred_element_type=jnp.float32)
    hidden = (jax.nn.silu(gate) * up).astype(jnp.bfloat16)
    down_whole = lax.all_gather(down_weight.T, axes, axis=0, tiled=True)
    contract = (((1,), (1,)), ((), ()))
    branch = lax.dot_general(hidden, down_whole, contract, preferred_element_type=jnp.float32)
    head_input = layer_norm(inputs + branch, head_gain).astype(jnp.bfloat16)
    return lax.dot_general(head, head_input, contract, preferred_element_type=jnp.float32)


def on_device(
    tokens,
    ln_gain,
    gate_weight,
    up_weight,
    down_weight,
    head_gain,
    depth_weight,
    context_weight,
    slot_point,
    slot_cell,
    slot_count,
    conv1_weight,
    conv1_bias,
    conv2_weight,
    conv2_bias,
):
    tiles, cams = lax.axis_size("tile"), lax.axis_size("cam")
    token_count, width = tokens.shape
    bins, channels = depth_weight.shape[1], context_weight.shape[1]
    slots = packed_slots(slot_point, slot_cell, slot_count, token_count * bins)
    weights = [
        conv1_weight.reshape(3, 3 * channels, channels),
        conv1_bias.reshape(1, channels),
        conv2_weight.reshape(3, 3 * channels, channels),
        conv2_bias.reshape(1, channels),
    ]
    head = jnp.concatenate([depth_weight, context_weight], axis=1).T
    sizes = (tiles, bins, channels, token_count)
    rows, units = gate_weight.shape
    fused = cams == 4 and tiles % 2 == 0 and rows % 16 == 0 and (rows * tiles) % LANES == 0
    if not fused:
        scores = table_of(
            tokens, ln_gain, gate_weight, up_weight, down_weight, head_gain, head
        )
        return run(False, [soft_table(scores, bins)], slots, weights, sizes)
    stacked = jnp.stack([gate_weight, up_weight, down_weight.T], axis=0)
    stacked = jnp.pad(stacked, ((0, 0), (0, 0), (0, -units % (2 * LANES))))
    own = stacked.reshape(3, rows, 2, -1).transpose(2, 0, 1, 3)
    arrays = [tokens, ln_gain.reshape(1, width), own, head_gain.reshape(1, width), head]
    return run(True, arrays, slots, weights, sizes)


def solution(mesh):
    return jax.shard_map(
        on_device,
        mesh=mesh,
        in_specs=(
            P(("cam", "tile"), None),
            P(),
            P(("cam", "tile"), None),
            P(("cam", "tile"), None),
            P(None, ("cam", "tile")),
            P(),
            P(),
            P(),
            P(("cam", "tile"), None, None),
            P(("cam", "tile"), None, None),
            P(("cam", "tile"), None),
            P(),
            P(),
            P(),
            P(),
        ),
        out_specs=P("cam", "tile", None, None),
        check_vma=False,
    )
```

time: 295 us -> 121 us (0.41)
  waiting for transfers between devices: 202 us -> 0 us
  Pallas kernels: 34.9 us -> 115 us
  matrix products: 19.3 us -> 0 us
  starting transfers between devices: 14.1 us -> 0 us
  between operations: 13.5 us -> 0.05 us
  other arithmetic: 6.3 us -> 1.99 us
    all_gather x3 -> x0, waiting for transfers between devices: 186 us -> none  [the longest x1 68.9 us: on_device(): lax.all_gather(down_weight.T, ('cam', 'tile'), axis=0, tiled=True)]
    pallas_call x1, Pallas kernels: 34.9 us -> 115 us  [run(): pl.pallas_call(functools.partial(program, fused, tiles, bins), out_shape=...]
    dot_general x22 -> x0, matrix products: 19.3 us -> none  [the longest x1 7.89 us: on_device(): lax.dot_general(hidden, down_whole, (((1,), (1,)), ((), ())), preferred_e...]
    ppermute x2 -> x0, waiting for transfers between devices: 8.49 us -> none  [the longest x1 8.49 us: extended_2(): before = lax.ppermute(last, axis, up)]
    all_to_all x1 -> x0, starting transfers between devices: 7.28 us -> none  [slot_rows(): lax.all_to_all(packed, 'tile', split_axis=0, concat_axis=0, tiled=True)]
    ppermute x2 -> x0, starting transfers between devices: 6.75 us -> none  [the longest x1 5.28 us: extended_2(): before = lax.ppermute(last, axis, up)]
    all_to_all x1 -> x0, waiting for transfers between devices: 4.69 us -> none  [slot_rows(): lax.all_to_all(packed, 'tile', split_axis=0, concat_axis=0, tiled=True)]
  transfers between devices with their start and end apart: 6 -> 0, of which waited for: 5 -> 0; matrix products, arithmetic and copies ran while one was open for 4% -> 0% of each run, Pallas kernels for 0% -> 0%
where the time goes in v1:
time: 121 us
  Pallas kernels  115 us (95%)
  local copies, waits for them, and re-layouts  3.68 us (3%)
  other arithmetic  1.99 us (2%)
    pallas_call x1, Pallas kernels, run(): pl.pallas_call(functools.partial(program, fused, tiles, bins), out_shape=...  115 us

profile of v1, /device:TPU:0, one launch (start us, length us, event | category | flops | bytes accessed | tf_op | source)
XLA Modules:
  0.0 120.9 jit_solution(15866527096512587034)
XLA Ops:
  0.0 1.1 fusion.4
  1.1 0.0 copy-start
  1.2 0.0 copy-start.1
  1.2 0.8 copy.21
  2.0 0.1 copy-done
  2.1 0.0 copy-start.2
  2.1 0.0 copy-start.3
  2.1 0.0 copy-start.4
  2.1 0.1 copy.18
  2.3 0.0 copy-done.1
  2.3 0.8 maximum_bitcast_fusion.refs_4_
  3.0 0.0 copy-done.2
  3.0 0.0 copy-done.3
  3.0 0.0 copy-done.4
  3.0 0.1 bitcast_add_fusion
  3.2 0.7 reshape.37.refs_5_
  3.8 115.2 %shard_map.145 = bf16[2,4,256,128]{3,2,1,0:T(8,128)(2,1)} custom-call(bf16[176,1024]{1,0:T(8,128)(2,1)} %refs_0_.1, f32[1,1024]{1,0:T(1,128)} %bitcast.36, bf16[2,3,32,1408]{3,2,1,0:T(8,128)(2,1)} %bitcast.29, f32[1,1024]{1,0:T(1,128)} %bitcast.37, bf16[192,1024]{1,0:T(8,128)(2,1)} %maximum_bitcast_fusion.refs_4_, s32[8,1,2560]{2,1,0:T(1,128)} %reshape.37.refs_5_, ...), custom_call_target="tpu_custom_call" | custom-call | tf_op jit(solution)/shard_map/pallas_call | solution.py:535
  119.0 1.9 %copy.23 = bf16[2,4,256,128]{3,2,1,0:T(8,128)(2,1)} copy(bf16[2,4,256,128]{3,2,1,0:T(8,128)(2,1)} %shard_map.145) | data formatting | bytes 1048576
  (1 shorter events, 0.0 us)
Async XLA Ops:
  1.1 1.0 copy-start
  1.2 1.1 copy-start.1
  2.1 0.9 copy-start.2
  2.1 0.9 copy-start.3
  2.1 0.9 copy-start.4

commit v2 on v1

v2 whole, which is shorter than its diff:
```python
import functools

import jax
import jax.numpy as jnp
from jax import lax
from jax.experimental import pallas as pl
from jax.experimental.pallas import tpu as pltpu
from jax.sharding import PartitionSpec as P

ROWS_DEV = 4
GRID_W = 256
SCN = 2
CHUNK = 512
LANES = 128
MESH = pl.DeviceIdType.MESH


def layer_norm(values, gain):
    center = values - jnp.mean(values, axis=-1, keepdims=True)
    spread = jnp.mean(center * center, axis=-1, keepdims=True)
    return center * lax.rsqrt(spread + 1e-06) * gain


def remote(src, dst, send, recv, cam, tile):
    return pltpu.make_async_remote_copy(
        src_ref=src,
        dst_ref=dst,
        send_sem=send,
        recv_sem=recv,
        device_id={"cam": cam, "tile": tile},
        device_id_type=MESH,
    )


def soft_table(scores, bins):
    logits = scores[:bins]
    top = jnp.max(logits, axis=0, keepdims=True)
    raised = jnp.exp(logits - top)
    depth = raised / jnp.sum(raised, axis=0, keepdims=True)
    return jnp.concatenate([depth, scores[bins:]], axis=0).astype(jnp.bfloat16)


class Exchange:
    SPAN = ((0, 1), (1, 1), (2, 1), (0, 2))

    def __init__(self, tiles, own, whole, recv, sends):
        self.cam, self.tile = lax.axis_index("cam"), lax.axis_index("tile")
        self.tiles, self.depth = tiles, tiles // 2
        self.y, self.c = self.cam // 2, lax.rem(self.cam, 2)
        self.z, self.x = self.tile // 2, lax.rem(self.tile, 2)
        self.own, self.whole, self.recv = own, whole, recv
        self.up, self.down, self.side, self.core, self.pair = sends
        self.rows = own.shape[2]

    def shard(self, y, c, z, x):
        return (2 * y + c) * self.tiles + 2 * z + x

    def block(self, kind, shard):
        first, count = self.SPAN[kind]
        rows = pl.ds(pl.multiple_of(shard * self.rows, self.rows), self.rows)
        return self.whole.at[pl.ds(first, count), rows, :]

    def mine(self, kind, half):
        first, count = self.SPAN[kind]
        return self.own.at[half, pl.ds(first, count)]

    def to(self, route, kind, y, z, x):
        shard = self.shard(y, self.c, z, x)
        block = self.block(kind, shard)
        at = (kind, y, 2 * z + x)
        got = self.recv.at[kind, shard]
        if route == "up":
            return remote(block, block, self.up.at[at], got, self.cam, self.tile + 2)
        if route == "down":
            return remote(block, block, self.down.at[at], got, self.cam, self.tile - 2)
        if route == "side":
            other = 2 * (1 - self.y) + self.c
            return remote(block, block, self.side.at[at], got, other, self.tile)
        other = 2 * self.y + 1 - self.c
        return remote(block, block, self.core.at[at], got, other, self.tile)

    def across(self, kind):
        shard = self.shard(self.y, self.c, self.z, self.x)
        return remote(
            self.mine(kind, 1 - self.x),
            self.block(kind, shard),
            self.pair.at[kind],
            self.recv.at[kind, shard],
            self.cam,
            self.tile + 1 - 2 * self.x,
        )

    def wait(self, kind, y, c, z, x):
        shard = self.shard(y, c, z, x)
        block = self.block(kind, shard)
        remote(
            block, block, self.pair.at[kind], self.recv.at[kind, shard], self.cam, self.tile
        ).wait_recv()

    def spread(self, kind, y, x, side):
        def go_up():
            self.to("up", kind, y, self.z, x).start()

        def go_down():
            self.to("down", kind, y, self.z, x).start()

        if side:
            self.to("side", kind, y, self.z, x).start()
        pl.when(self.z + 1 < self.depth)(go_up)
        pl.when(self.z > 0)(go_down)
        self.to("core", kind, y, self.z, x).start()

    def units(self, late):
        mate = 1 - self.x
        if late:
            return ((2, self.y, self.x, True), (2, self.y, mate, True))
        return (
            (0, self.y, self.x, True),
            (1, self.y, self.x, False),
            (1, 1 - self.y, self.x, False),
            (3, self.y, mate, True),
        )

    def relay(self, late, d):
        def take(kind, y, z, x, side, more, route):
            self.wait(kind, y, self.c, z, x)
            if d + 1 < self.depth:
                pl.when(more)(lambda: self.to(route, kind, y, z, x).start())
            if side:
                self.to("side", kind, y, z, x).start()
            self.to("core", kind, y, z, x).start()

        for kind, y, x, side in self.units(late):

            def below():
                take(kind, y, self.z - d, x, side, self.z + 1 < self.depth, "up")

            def above():
                take(kind, y, self.z + d, x, side, self.z > 0, "down")

            pl.when(self.z - d >= 0)(below)
            pl.when(self.z + d < self.depth)(above)

    def crossed(self, late, z):
        for kind, y, x, side in self.units(late):
            if side:
                self.wait(kind, 1 - self.y, self.c, z, x)
                self.to("core", kind, 1 - self.y, z, x).start()

    def crossed_at(self, late, d):
        pl.when(self.z - d >= 0)(lambda: self.crossed(late, self.z - d))
        pl.when(self.z + d < self.depth)(lambda: self.crossed(late, self.z + d))

    def beside(self, late, y, zs):
        for z in zs:
            if late:
                for x in range(2):
                    self.wait(2, y, 1 - self.c, z, x)
            else:
                self.wait(0, y, 1 - self.c, z, self.x)
                self.wait(1, y, 1 - self.c, z, self.x)
                self.wait(3, y, 1 - self.c, z, 1 - self.x)

    def finish(self):
        self.across(3).wait_send()
        self.across(2).wait_send()
        for z in range(self.depth):
            for kind, y, x, side in (*self.units(False), *self.units(True)):

                def up():
                    self.to("up", kind, y, z, x).wait_send()

                def down():
                    self.to("down", kind, y, z, x).wait_send()

                pl.when((self.z >= z) & (self.z + 1 < self.depth))(up)
                pl.when((self.z <= z) & (self.z > 0))(down)
                self.to("core", kind, y, z, x).wait_send()
                if side:
                    self.to("side", kind, y, z, x).wait_send()
                    self.to("core", kind, 1 - y, z, x).wait_send()
        self.to("side", 1, self.y, self.z, self.x).wait_send()


def feed_forward(ex, tokens, gain, guest, normed, gate, up, hidden, kept, sent, came, sems, midway):
    local, tok_send, tok_recv, part_send, part_recv = sems
    count = tokens.shape[0]
    mate = ex.tile + 1 - 2 * ex.x
    token_copy = remote(tokens, guest, tok_send, tok_recv, ex.cam, mate)
    me = ex.shard(ex.y, ex.c, ex.z, ex.x)
    copies = [
        pltpu.make_async_copy(ex.mine(kind, ex.x), ex.block(kind, me), local.at[kind - 2])
        for kind in (3, 2)
    ]
    ex.across(3).start()
    for copy in copies:
        copy.start()
    copies[0].wait()
    ex.to("side", 1, ex.y, ex.z, ex.x).start()
    ex.spread(0, ex.y, ex.x, True)
    ex.spread(1, ex.y, ex.x, False)
    ex.across(2).start()
    token_copy.start()
    ex.wait(1, 1 - ex.y, ex.c, ex.z, ex.x)
    ex.spread(1, 1 - ex.y, ex.x, False)
    ex.wait(3, ex.y, ex.c, ex.z, 1 - ex.x)
    ex.spread(3, ex.y, 1 - ex.x, True)
    ex.relay(False, 1)
    ex.crossed(False, ex.z)
    for d in range(2, ex.depth - 1):
        ex.relay(False, d)
        ex.crossed_at(False, d - 1)
    copies[1].wait()
    ex.spread(2, ex.y, ex.x, True)
    ex.wait(2, ex.y, ex.c, ex.z, 1 - ex.x)
    ex.spread(2, ex.y, 1 - ex.x, True)
    token_copy.wait_recv()
    normed[count:] = layer_norm(guest[...].astype(jnp.float32), gain[...]).astype(jnp.bfloat16)
    wide = ex.rows * ex.tiles
    pieces = wide // LANES
    per_piece = ex.depth // pieces

    def project(cam, first):
        rows = pl.ds(pl.multiple_of(cam * wide, wide), wide)
        for which, total in ((0, gate), (1, up)):
            got = jnp.dot(
                normed[:, rows], ex.whole[which, rows, :], preferred_element_type=jnp.float32
            )
            if first:
                total[...] = got
            else:
                total[...] += got

    def part(piece):
        return remote(
            sent.at[piece], came.at[piece], part_send.at[piece], part_recv.at[piece], ex.cam, mate
        )

    def columns(cam, near):
        piece = cam * pieces + near
        rows = pl.ds(pl.multiple_of(piece * LANES, LANES), LANES)
        got = lax.dot_general(
            hidden[...],
            ex.whole[2, rows, :],
            (((1,), (1,)), ((), ())),
            preferred_element_type=jnp.float32,
        )
        kept[piece] = got[:count]
        sent[piece] = got[count:]
        part(piece).start()

    every = range(ex.depth)
    ex.relay(False, ex.depth - 1)
    midway()
    project(2 * ex.y + ex.c, True)
    ex.crossed_at(False, ex.depth - 2)
    ex.relay(True, 1)
    ex.beside(False, ex.y, every)
    project(2 * ex.y + 1 - ex.c, False)
    ex.crossed_at(False, ex.depth - 1)
    project(2 * (1 - ex.y) + ex.c, False)
    for d in range(2, ex.depth - 1):
        ex.relay(True, d)
    ex.beside(False, 1 - ex.y, every)
    project(2 * (1 - ex.y) + 1 - ex.c, False)
    value = gate[...]
    hidden[...] = (value / (1.0 + jnp.exp(-value)) * up[...]).astype(jnp.bfloat16)
    for turn in range(pieces):
        near = lax.rem(ex.z // per_piece + turn, pieces)
        zs = [near * per_piece + i for i in range(per_piece)]
        if turn == pieces - 1:
            ex.relay(True, ex.depth - 1)
        columns(2 * ex.y + ex.c, near)
        ex.beside(True, ex.y, zs)
        columns(2 * ex.y + 1 - ex.c, near)
        for z in zs:
            ex.crossed(True, z)
        columns(2 * (1 - ex.y) + ex.c, near)
        ex.beside(True, 1 - ex.y, zs)
        columns(2 * (1 - ex.y) + 1 - ex.c, near)
    for piece in range(kept.shape[0]):
        part(piece).wait_recv()
    blocks = [kept[piece] + came[piece] for piece in range(kept.shape[0])]
    updated = tokens[...].astype(jnp.float32) + jnp.concatenate(blocks, axis=1)

    def finish():
        token_copy.wait_send()
        for piece in range(kept.shape[0]):
            part(piece).wait_send()
        ex.finish()

    return updated, finish


def splat(held, slots, total, bins, sources, between):
    half = total.shape[0]
    tokens = held.shape[2]
    chunks = slots.shape[2] // CHUNK
    total[...] = jnp.zeros_like(total)

    def one_source(source):
        def step(i, inner):
            start = pl.multiple_of(i * CHUNK, CHUNK)
            packed = slots[source, :, pl.ds(start, CHUNK)]
            point, cell = packed // 65536, packed % 65536
            token, depth_bin = point // bins, point % bins
            token_ids = lax.broadcasted_iota(jnp.int32, (tokens, CHUNK), 0)
            pick = jnp.where(token_ids == token, 1.0, 0.0).astype(jnp.bfloat16)
            got = jnp.dot(held[source], pick, preferred_element_type=jnp.float32)
            bin_ids = lax.broadcasted_iota(jnp.int32, (bins, CHUNK), 0)
            weight = jnp.sum(
                jnp.where(bin_ids == depth_bin, got[:bins], 0.0), axis=0, keepdims=True
            )
            upper = cell >= half
            low = jnp.where(upper, 0.0, weight) * got[bins:]
            high = jnp.where(upper, weight, 0.0) * got[bins:]
            lifted = jnp.concatenate([low, high], axis=0).astype(jnp.bfloat16)
            local = jnp.where(upper, cell - half, cell)
            cell_ids = lax.broadcasted_iota(jnp.int32, (half, CHUNK), 0)
            place = jnp.where(cell_ids == local, 1.0, 0.0).astype(jnp.bfloat16)
            total[...] += lax.dot_general(
                place, lifted, (((1,), (1,)), ((), ())), preferred_element_type=jnp.float32
            )
            return inner

        lax.fori_loop(0, chunks, step, 0)

    for turn, source in enumerate(sources):
        between(turn, source)
        one_source(source)


class Tables:
    def __init__(self, tiles, table, held, sends, recv):
        self.cam, self.tile = lax.axis_index("cam"), lax.axis_index("tile")
        self.depth = tiles // 2
        self.z, self.x = self.tile // 2, lax.rem(self.tile, 2)
        self.table, self.held, self.recv = table, held, recv
        self.up, self.down, self.pair = sends

    def to(self, route, z):
        source = 2 * z + self.x
        dst = self.held.at[source]
        src = dst
        got = self.recv.at[source]
        if route == "up":
            return remote(src, dst, self.up.at[z], got, self.cam, self.tile + 2)
        if route == "down":
            return remote(src, dst, self.down.at[z], got, self.cam, self.tile - 2)
        return remote(src, dst, self.pair.at[z], got, self.cam, self.tile + 1 - 2 * self.x)

    def wait(self, source):
        dst = self.held.at[source]
        remote(dst, dst, self.pair.at[0], self.recv.at[source], self.cam, self.tile).wait_recv()

    def begin(self):
        pl.when(self.z + 1 < self.depth)(lambda: self.to("up", self.z).start())
        pl.when(self.z > 0)(lambda: self.to("down", self.z).start())
        self.to("pair", self.z).start()

    def relay(self, d):
        def take(z, more, route):
            self.wait(2 * z + self.x)
            pl.when(more)(lambda: self.to(route, z).start())
            self.to("pair", z).start()

        up, down = self.z + 1 < self.depth, self.z > 0
        pl.when(self.z - d >= 0)(lambda: take(self.z - d, up, "up"))
        pl.when(self.z + d < self.depth)(lambda: take(self.z + d, down, "down"))

    def place(self, turn):
        if self.depth & (self.depth - 1) == 0:
            return self.z ^ turn
        return lax.rem(self.z + turn, self.depth)

    def sources(self):
        found = []
        for turn in range(self.depth):
            found += [2 * self.place(turn) + self.x, 2 * self.place(turn) + 1 - self.x]
        return found

    def between(self, turn, source):
        if 0 < turn < self.depth:
            self.relay(turn)
        if turn % 2 == 1:
            self.wait(source)

    def finish(self):
        for z in range(self.depth):
            up = (self.z >= z) & (self.z + 1 < self.depth)
            pl.when(up)(lambda: self.to("up", z).wait_send())
            pl.when((self.z <= z) & (self.z > 0))(lambda: self.to("down", z).wait_send())
            self.to("pair", z).wait_send()


def fill_slots(point, cell, count, slots, points):
    tiles, _, width = slots.shape
    used = point.shape[2]
    ids = lax.broadcasted_iota(jnp.int32, (1, used), 1)
    for k in range(tiles):
        if used < width:
            slots[k] = jnp.full((1, width), points * 65536, jnp.int32)
        live = ids < count[0, k]
        row = jnp.where(live, point[0, k : k + 1, :], points) * 65536
        slots[k, :, :used] = row + cell[0, k : k + 1, :]


def fill_own(gate, up, down, own):
    units = gate.shape[1]
    width = own.shape[3]
    even = units - units % LANES
    for half in range(2):
        first = half * width
        full = min(width, even - first)
        for which, ref in ((0, gate), (1, up), (2, None)):

            def taken(start, size):
                if ref is None:
                    rows = down[start : start + size, :].astype(jnp.float32)
                    return jnp.transpose(rows).astype(jnp.bfloat16)
                return ref[:, start : start + size]

            own[half, which, :, :full] = taken(first, full)
            if full < width:
                rest = units - first - full
                blank = jnp.zeros((own.shape[2], width - full), jnp.bfloat16)
                own[half, which, :, full:] = blank
                if rest > 0:
                    own[half, which, :, full : full + rest] = taken(first + full, rest)


def widen(source, index, wide, row):
    value = source[index].astype(jnp.float32)
    columns, channels = value.shape
    places = lax.broadcasted_iota(jnp.int32, (columns, channels), 0)
    left = jnp.where(places == 0, 0.0, pltpu.roll(value, 1, 0))
    right = jnp.where(places == columns - 1, 0.0, pltpu.roll(value, columns - 1, 0))
    wide[row] = jnp.concatenate([left, value, right], axis=1).astype(jnp.bfloat16)


def convolve(wide, row, weight):
    total = None
    for shift in range(3):
        taps = weight[shift].reshape(wide.shape[2], -1)
        got = jnp.dot(wide[row + shift], taps, preferred_element_type=jnp.float32)
        total = got if total is None else total + got
    return total


def program(fused, tiles, bins, *refs):
    if fused:
        (tokens, gain, w_gate, w_up, w_down, head_gain, w_depth, w_context) = refs[:8]
        (point, cell, live, w1, b1, w2, b2, out) = refs[8:16]
        refs = refs[16:]
    else:
        (table_in, point, cell, live, w1, b1, w2, b2, out) = refs[:9]
        refs = refs[9:]
    (slot_in, slots, held, total, ext, wide, mid, wide_mid) = refs[:8]
    (slot_send, slot_recv, t_up, t_down, t_pair, t_recv, halo_send, halo_recv) = refs[8:16]
    if fused:
        (own, whole, guest, normed, gate, up, hidden, kept, sent, came) = refs[16:26]
        (recv, zup, zdown, side, core, pair) = refs[26:32]
        sems = refs[32:37]
    cam, me = lax.axis_index("cam"), lax.axis_index("tile")
    token_count = held.shape[2]
    barrier = pltpu.get_barrier_semaphore()

    def hello(other_cam, other_tile):
        pl.semaphore_signal(
            barrier, inc=1, device_id={"cam": other_cam, "tile": other_tile}, device_id_type=MESH
        )

    if fused:
        y, c = cam // 2, lax.rem(cam, 2)
        before, after = me >= 2, me + 2 < tiles
        hello(2 * y + 1 - c, me)
        hello(2 * (1 - y) + c, me)
        hello(cam, me + 1 - 2 * lax.rem(me, 2))
        pl.when(before)(lambda: hello(cam, me - 2))
        pl.when(after)(lambda: hello(cam, me + 2))
        expected = 3 + jnp.where(before, 1, 0) + jnp.where(after, 1, 0)
        fill_own(w_gate, w_up, w_down, own)
        normed[:token_count] = layer_norm(tokens[...].astype(jnp.float32), gain[...]).astype(
            jnp.bfloat16
        )
    else:

        def greet(k, carry):
            hello(cam, lax.rem(me + k, tiles))
            return carry

        lax.fori_loop(1, tiles, greet, 0)
        expected = tiles - 1
    fill_slots(point, cell, live, slot_in, token_count * bins)
    pl.semaphore_wait(barrier, expected)

    def slot_copy(k):
        other = lax.rem(me + k, tiles)
        return remote(slot_in.at[other], slots.at[me], slot_send.at[k], slot_recv.at[k], cam, other)

    def slot_wait(k):
        source = lax.rem(me - k + tiles, tiles)
        remote(
            slot_in.at[me], slots.at[source], slot_send.at[k], slot_recv.at[k], cam, me
        ).wait_recv()

    def slot_start(k, carry):
        slot_copy(k).start()
        return carry

    def slot_finish(k, carry):
        slot_wait(k)
        slot_copy(k).wait_send()
        return carry

    own_slots = pltpu.make_async_copy(slot_in.at[me], slots.at[me], slot_send.at[0])

    def send_slots():
        lax.fori_loop(1, tiles, slot_start, 0)
        own_slots.start()

    if fused:
        ex = Exchange(tiles, own, whole, recv, (zup, zdown, side, core, pair))
        updated, finish = feed_forward(
            ex, tokens, gain, guest, normed, gate, up, hidden, kept, sent, came, sems, send_slots
        )
        head_input = layer_norm(updated, head_gain[...]).astype(jnp.bfloat16)
        scores = [
            jnp.transpose(jnp.dot(head_input, weight[...], preferred_element_type=jnp.float32))
            for weight in (w_depth, w_context)
        ]
        held[me] = soft_table(jnp.concatenate(scores, axis=0), bins)
    else:
        send_slots()
        held[me] = table_in[...]
    tables = Tables(tiles, None, held, (t_up, t_down, t_pair), t_recv)
    tables.begin()
    own_slots.wait()
    lax.fori_loop(1, tiles, slot_finish, 0)
    splat(held, slots, total, bins, tables.sources(), tables.between)
    channels = total.shape[1] // 2
    per_scene = ROWS_DEV * GRID_W
    for scene in range(SCN):
        for row in range(ROWS_DEV):
            start = scene * per_scene + row * GRID_W
            side_of, first = divmod(start, total.shape[0])
            ext[scene, 2 + row] = total[
                first : first + GRID_W, side_of * channels : (side_of + 1) * channels
            ].astype(jnp.bfloat16)

    def halo(which):
        if which == 0:
            src, dst, other = ext.at[:, 2:4], ext.at[:, ROWS_DEV + 2 : ROWS_DEV + 4], me - 1
        else:
            src, dst, other = ext.at[:, ROWS_DEV : ROWS_DEV + 2], ext.at[:, 0:2], me + 1
        return remote(src, dst, halo_send.at[which], halo_recv.at[which], cam, other)

    blank = jnp.zeros((SCN, 2, GRID_W, channels), jnp.bfloat16)

    def first_tile():
        ext[:, 0:2] = blank

    def last_tile():
        ext[:, ROWS_DEV + 2 : ROWS_DEV + 4] = blank

    has_before, has_after = me > 0, me + 1 < tiles
    pl.when(has_before)(lambda: halo(0).start())
    pl.when(has_after)(lambda: halo(1).start())
    pl.when(me == 0)(first_tile)
    pl.when(me + 1 == tiles)(last_tile)
    rows_ext = ROWS_DEV + 4
    for scene in range(SCN):
        for row in range(2, ROWS_DEV + 2):
            widen(ext, (scene, row), wide, scene * rows_ext + row)
    pl.when(has_before)(lambda: halo(1).wait_recv())
    pl.when(has_after)(lambda: halo(0).wait_recv())
    for scene in range(SCN):
        for row in (0, 1, ROWS_DEV + 2, ROWS_DEV + 3):
            widen(ext, (scene, row), wide, scene * rows_ext + row)
    rows_mid = ROWS_DEV + 2
    for scene in range(SCN):
        for row in range(rows_mid):
            value = jnp.maximum(convolve(wide, scene * rows_ext + row, w1) + b1[...], 0.0)
            if row == 0:
                value = jnp.where(has_before, value, 0.0)
            if row == rows_mid - 1:
                value = jnp.where(has_after, value, 0.0)
            mid[scene, row] = value.astype(jnp.bfloat16)
            widen(mid, (scene, row), wide_mid, scene * rows_mid + row)
    for scene in range(SCN):
        for row in range(ROWS_DEV):
            value = convolve(wide_mid, scene * rows_mid + row, w2) + b2[...]
            value = ext[scene, 2 + row].astype(jnp.float32) + value
            out[scene, row] = value.astype(jnp.bfloat16)
    pl.when(has_before)(lambda: halo(0).wait_send())
    pl.when(has_after)(lambda: halo(1).wait_send())
    tables.finish()
    if fused:
        finish()


def run(fused, arrays, slots, weights, sizes):
    tiles, bins, channels, token_count = sizes
    cells = SCN * ROWS_DEV * GRID_W
    dma = pltpu.SemaphoreType.DMA
    bf16, f32 = jnp.bfloat16, jnp.float32
    slot_count = slots[0].shape[2]
    slot_width = slot_count + -slot_count % CHUNK
    scratch = [
        pltpu.VMEM((tiles, 1, slot_width), jnp.int32),
        pltpu.VMEM((tiles, 1, slot_width), jnp.int32),
        pltpu.VMEM((tiles, bins + channels, token_count), bf16),
        pltpu.VMEM((cells // 2, 2 * channels), f32),
        pltpu.VMEM((SCN, ROWS_DEV + 4, GRID_W, channels), bf16),
        pltpu.VMEM((SCN * (ROWS_DEV + 4), GRID_W, 3 * channels), bf16),
        pltpu.VMEM((SCN, ROWS_DEV + 2, GRID_W, channels), bf16),
        pltpu.VMEM((SCN * (ROWS_DEV + 2), GRID_W, 3 * channels), bf16),
        dma((tiles,)),
        dma((tiles,)),
        dma((tiles // 2,)),
        dma((tiles // 2,)),
        dma((tiles // 2,)),
        dma((tiles,)),
        dma((2,)),
        dma((2,)),
    ]
    operands = [*arrays, *slots, *weights]
    specs = [pl.BlockSpec(memory_space=pltpu.VMEM)] * len(operands)
    specs[len(arrays) + 2] = pl.BlockSpec(memory_space=pltpu.SMEM)
    if fused:
        tokens, gate_weight = arrays[0], arrays[2]
        count, width = tokens.shape
        rows, units = gate_weight.shape
        cams = lax.axis_size("cam")
        half = (units + -units % (2 * LANES)) // 2
        pieces = width // LANES
        scratch += [
            pltpu.VMEM((2, 3, rows, half), bf16),
            pltpu.VMEM((3, width, half), bf16),
            pltpu.VMEM((count, width), bf16),
            pltpu.VMEM((2 * count, width), bf16),
            pltpu.VMEM((2 * count, half), f32),
            pltpu.VMEM((2 * count, half), f32),
            pltpu.VMEM((2 * count, half), bf16),
            pltpu.VMEM((pieces, count, LANES), f32),
            pltpu.VMEM((pieces, count, LANES), f32),
            pltpu.VMEM((pieces, count, LANES), f32),
            dma((4, cams * tiles)),
            dma((4, 2, tiles)),
            dma((4, 2, tiles)),
            dma((4, 2, tiles)),
            dma((4, 2, tiles)),
            dma((4,)),
            dma((2,)),
            dma,
            dma,
            dma((pieces,)),
            dma((pieces,)),
        ]
    return pl.pallas_call(
        functools.partial(program, fused, tiles, bins),
        out_shape=jax.ShapeDtypeStruct((SCN, ROWS_DEV, GRID_W, channels), bf16),
        in_specs=specs,
        out_specs=pl.BlockSpec(memory_space=pltpu.VMEM),
        scratch_shapes=scratch,
        compiler_params=pltpu.CompilerParams(
            collective_id=0, has_side_effects=True, vmem_limit_bytes=60 * 1024 * 1024
        ),
    )(*operands)


def table_of(tokens, ln_gain, gate_weight, up_weight, down_weight, head_gain, head):
    inputs = tokens.astype(jnp.float32)
    normed = layer_norm(inputs, ln_gain).astype(jnp.bfloat16)
    axes = ("cam", "tile")
    gate_whole = lax.all_gather(gate_weight, axes, axis=0, tiled=True)
    up_whole = lax.all_gather(up_weight, axes, axis=0, tiled=True)
    gate = jnp.dot(normed, gate_whole, preferred_element_type=jnp.float32)
    up = jnp.dot(normed, up_whole, preferred_element_type=jnp.float32)
    hidden = (jax.nn.silu(gate) * up).astype(jnp.bfloat16)
    down_whole = lax.all_gather(down_weight.T, axes, axis=0, tiled=True)
    contract = (((1,), (1,)), ((), ()))
    branch = lax.dot_general(hidden, down_whole, contract, preferred_element_type=jnp.float32)
    head_input = layer_norm(inputs + branch, head_gain).astype(jnp.bfloat16)
    return lax.dot_general(head, head_input, contract, preferred_element_type=jnp.float32)


def on_device(
    tokens,
    ln_gain,
    gate_weight,
    up_weight,
    down_weight,
    head_gain,
    depth_weight,
    context_weight,
    slot_point,
    slot_cell,
    slot_count,
    conv1_weight,
    conv1_bias,
    conv2_weight,
    conv2_bias,
):
    tiles, cams = lax.axis_size("tile"), lax.axis_size("cam")
    token_count, width = tokens.shape
    bins, channels = depth_weight.shape[1], context_weight.shape[1]
    slots = [slot_point, slot_cell, slot_count]
    weights = [
        conv1_weight,
        conv1_bias.reshape(1, channels),
        conv2_weight,
        conv2_bias.reshape(1, channels),
    ]
    sizes = (tiles, bins, channels, token_count)
    rows, units = gate_weight.shape
    fused = cams == 4 and tiles % 4 == 0 and rows % 16 == 0 and (rows * tiles) % LANES == 0
    if not fused:
        head = jnp.concatenate([depth_weight, context_weight], axis=1).T
        scores = table_of(
            tokens, ln_gain, gate_weight, up_weight, down_weight, head_gain, head
        )
        return run(False, [soft_table(scores, bins)], slots, weights, sizes)
    arrays = [
        tokens,
        ln_gain.reshape(1, width),
        gate_weight,
        up_weight,
        down_weight,
        head_gain.reshape(1, width),
        depth_weight,
        context_weight,
    ]
    return run(True, arrays, slots, weights, sizes)


def solution(mesh):
    return jax.shard_map(
        on_device,
        mesh=mesh,
        in_specs=(
            P(("cam", "tile"), None),
            P(),
            P(("cam", "tile"), None),
            P(("cam", "tile"), None),
            P(None, ("cam", "tile")),
            P(),
            P(),
            P(),
            P(("cam", "tile"), None, None),
            P(("cam", "tile"), None, None),
            P(("cam", "tile"), None),
            P(),
            P(),
            P(),
            P(),
        ),
        out_specs=P("cam", "tile", None, None),
        check_vma=False,
    )
```

time: 121 us -> 116 us (0.959)
  the two profiles are of different devices: /device:TPU:0 before, /device:TPU:17 now
where the time goes in v2:
time: 116 us
  Pallas kernels  111 us (96%)
  local copies, waits for them, and re-layouts  4.79 us (4%)
    pallas_call x1, Pallas kernels, run(): pl.pallas_call(functools.partial(program, fused, tiles, bins), out_shape=...  111 us
    unnamed x5, local copies, waits for them, and re-layouts  4.79 us

profile of v2, /device:TPU:17, one launch (start us, length us, event | category | flops | bytes accessed | tf_op | source)
XLA Modules:
  0.0 116.3 jit_solution(10590389773485998971)
XLA Ops:
  0.0 0.0 copy-start
  0.0 1.8 %copy.17.refs_6_ = bf16[1024,64]{1,0:T(8,128)(2,1)} copy(bf16[1024,64]{0,1:T(8,128)(2,1)} %param.21) | data formatting | bytes 262144 | tf_op args[6]
  1.8 0.0 copy-done
  1.8 1.1 copy.16.refs_4_
  2.9 111.5 %shard_map.145 = bf16[2,4,256,128]{3,2,1,0:T(8,128)(2,1)} custom-call(bf16[176,1024]{1,0:T(8,128)(2,1)} %refs_0_.1, f32[1,1024]{1,0:T(1,128)} %bitcast.4, bf16[32,2730]{1,0:T(8,128)(2,1)} %refs_2_.1, bf16[32,2730]{1,0:T(8,128)(2,1)} %refs_3_.1, bf16[2730,32]{1,0:T(8,128)(2,1)} %copy.16.refs_4_, f32[1,1024]{1,0:T(1,128)} %bitcast.5, ...), custom_call_target="tpu_custom_call" | custom-call | tf_op jit(solution)/shard_map/pallas_call | solution.py:660
  114.4 1.9 %copy.19 = bf16[2,4,256,128]{3,2,1,0:T(8,128)(2,1)} copy(bf16[2,4,256,128]{3,2,1,0:T(8,128)(2,1)} %shard_map.145) | data formatting | bytes 1048576
Async XLA Ops:
  0.0 1.8 %copy-start = (bf16[2730,32]{0,1:T(8,128)(2,1)S(1)}, bf16[2730,32]{0,1:T(8,128)(2,1)}, u32[]{:S(2)}) copy-start(bf16[2730,32]{0,1:T(8,128)(2,1)} %param.19) | copy-start | bytes 524164

commit v3 on v2

--- a/solution.py
+++ b/solution.py
@@ -10,7 +10,6 @@
 ROWS_DEV = 4
 GRID_W = 256
 SCN = 2
-CHUNK = 512
 LANES = 128
 MESH = pl.DeviceIdType.MESH
 
@@ -32,12 +31,22 @@
     )
 
 
-def soft_table(scores, bins):
-    logits = scores[:bins]
-    top = jnp.max(logits, axis=0, keepdims=True)
-    raised = jnp.exp(logits - top)
-    depth = raised / jnp.sum(raised, axis=0, keepdims=True)
-    return jnp.concatenate([depth, scores[bins:]], axis=0).astype(jnp.bfloat16)
+def soft_depth(logits):
+    raised = jnp.exp(logits - jnp.max(logits, axis=0, keepdims=True))
+    return raised / jnp.sum(raised, axis=0, keepdims=True)
+
+
+def table_of(depth, context):
+    bins, tokens = depth.shape
+    rows = [context.astype(jnp.bfloat16)]
+    depth = depth.astype(jnp.bfloat16)
+    for first in range(0, tokens, LANES):
+        block = depth[:, first : first + LANES]
+        if block.shape[1] < LANES:
+            blank = jnp.zeros((bins, LANES - block.shape[1]), jnp.bfloat16)
+            block = jnp.concatenate([block, blank], axis=1)
+        rows.append(block)
+    return jnp.concatenate(rows, axis=0)
 
 
 class Exchange:
@@ -292,50 +301,49 @@
     return updated, finish
 
 
-def splat(held, slots, total, bins, sources, between):
-    half = total.shape[0]
-    tokens = held.shape[2]
-    chunks = slots.shape[2] // CHUNK
-    total[...] = jnp.zeros_like(total)
-
-    def one_source(source):
-        def step(i, inner):
-            start = pl.multiple_of(i * CHUNK, CHUNK)
-            packed = slots[source, :, pl.ds(start, CHUNK)]
-            point, cell = packed // 65536, packed % 65536
-            token, depth_bin = point // bins, point % bins
-            token_ids = lax.broadcasted_iota(jnp.int32, (tokens, CHUNK), 0)
-            pick = jnp.where(token_ids == token, 1.0, 0.0).astype(jnp.bfloat16)
-            got = jnp.dot(held[source], pick, preferred_element_type=jnp.float32)
-            bin_ids = lax.broadcasted_iota(jnp.int32, (bins, CHUNK), 0)
-            weight = jnp.sum(
-                jnp.where(bin_ids == depth_bin, got[:bins], 0.0), axis=0, keepdims=True
-            )
-            upper = cell >= half
-            low = jnp.where(upper, 0.0, weight) * got[bins:]
-            high = jnp.where(upper, weight, 0.0) * got[bins:]
-            lifted = jnp.concatenate([low, high], axis=0).astype(jnp.bfloat16)
-            local = jnp.where(upper, cell - half, cell)
-            cell_ids = lax.broadcasted_iota(jnp.int32, (half, CHUNK), 0)
-            place = jnp.where(cell_ids == local, 1.0, 0.0).astype(jnp.bfloat16)
-            total[...] += lax.dot_general(
-                place, lifted, (((1,), (1,)), ((), ())), preferred_element_type=jnp.float32
-            )
-            return inner
-
-        lax.fori_loop(0, chunks, step, 0)
-
-    for turn, source in enumerate(sources):
-        between(turn, source)
-        one_source(source)
+def one_hot(count, index):
+    ids = lax.broadcasted_iota(jnp.int16, (count, index.shape[1]), 0)
+    one, zero = jnp.array(1, jnp.bfloat16), jnp.array(0, jnp.bfloat16)
+    return jnp.where(ids == index.astype(jnp.int16), one, zero)
+
+
+def lift(table, packed, tokens, bins):
+    point = packed // 65536
+    token, depth_bin = point // bins, point % bins
+    pick = one_hot(tokens, token)
+    blocks = []
+    for first in range(0, tokens, LANES):
+        row = tokens + first // LANES * bins
+        blocks.append(table[row : row + bins, : min(LANES, tokens - first)])
+    depth = jnp.concatenate(blocks, axis=1)
+    found = jnp.dot(depth, pick, preferred_element_type=jnp.float32)
+    bin_ids = lax.broadcasted_iota(jnp.int32, found.shape, 0)
+    weight = jnp.sum(jnp.where(bin_ids == depth_bin, found, 0.0), axis=0, keepdims=True)
+    context = lax.dot_general(
+        table[:tokens], pick, (((0,), (0,)), ((), ())), preferred_element_type=jnp.float32
+    )
+    return weight * context
+
+
+def add_scene(total, scene, lifted, packed):
+    half = total.shape[1]
+    cell = packed % 65536
+    part = cell // half
+    low = jnp.where(part == 2 * scene, lifted, 0.0)
+    high = jnp.where(part == 2 * scene + 1, lifted, 0.0)
+    both = jnp.concatenate([low, high], axis=0).astype(jnp.bfloat16)
+    place = one_hot(half, cell % half)
+    total[scene] += lax.dot_general(
+        place, both, (((1,), (1,)), ((), ())), preferred_element_type=jnp.float32
+    )
 
 
 class Tables:
-    def __init__(self, tiles, table, held, sends, recv):
+    def __init__(self, tiles, held, sends, recv):
         self.cam, self.tile = lax.axis_index("cam"), lax.axis_index("tile")
         self.depth = tiles // 2
         self.z, self.x = self.tile // 2, lax.rem(self.tile, 2)
-        self.table, self.held, self.recv = table, held, recv
+        self.held, self.recv = held, recv
         self.up, self.down, self.pair = sends
 
     def to(self, route, z):
@@ -368,22 +376,17 @@
         pl.when(self.z - d >= 0)(lambda: take(self.z - d, up, "up"))
         pl.when(self.z + d < self.depth)(lambda: take(self.z + d, down, "down"))
 
-    def place(self, turn):
+    def source(self, turn):
+        step = turn // 2
         if self.depth & (self.depth - 1) == 0:
-            return self.z ^ turn
-        return lax.rem(self.z + turn, self.depth)
-
-    def sources(self):
-        found = []
-        for turn in range(self.depth):
-            found += [2 * self.place(turn) + self.x, 2 * self.place(turn) + 1 - self.x]
-        return found
-
-    def between(self, turn, source):
-        if 0 < turn < self.depth:
-            self.relay(turn)
-        if turn % 2 == 1:
-            self.wait(source)
+            z = self.z ^ step
+        else:
+            z = lax.rem(self.z + step, self.depth)
+        return 2 * z + (self.x ^ lax.rem(turn, 2))
+
+    def between(self, turn):
+        pl.when((turn > 0) & (turn < self.depth))(lambda: self.relay(turn))
+        pl.when(lax.rem(turn, 2) == 1)(lambda: self.wait(self.source(turn)))
 
     def finish(self):
         for z in range(self.depth):
@@ -412,21 +415,15 @@
     for half in range(2):
         first = half * width
         full = min(width, even - first)
-        for which, ref in ((0, gate), (1, up), (2, None)):
-
-            def taken(start, size):
-                if ref is None:
-                    rows = down[start : start + size, :].astype(jnp.float32)
-                    return jnp.transpose(rows).astype(jnp.bfloat16)
-                return ref[:, start : start + size]
-
-            own[half, which, :, :full] = taken(first, full)
+        for which, ref in ((0, gate), (1, up), (2, down)):
+            own[half, which, :, :full] = ref[:, first : first + full]
             if full < width:
                 rest = units - first - full
                 blank = jnp.zeros((own.shape[2], width - full), jnp.bfloat16)
                 own[half, which, :, full:] = blank
                 if rest > 0:
-                    own[half, which, :, full : full + rest] = taken(first + full, rest)
+                    tail = ref[:, first + full : units]
+                    own[half, which, :, full : full + rest] = tail
 
 
 def widen(source, index, wide, row):
@@ -447,7 +444,7 @@
     return total
 
 
-def program(fused, tiles, bins, *refs):
+def program(fused, tiles, bins, token_count, *refs):
     if fused:
         (tokens, gain, w_gate, w_up, w_down, head_gain, w_depth, w_context) = refs[:8]
         (point, cell, live, w1, b1, w2, b2, out) = refs[8:16]
@@ -455,14 +452,13 @@
     else:
         (table_in, point, cell, live, w1, b1, w2, b2, out) = refs[:9]
         refs = refs[9:]
-    (slot_in, slots, held, total, ext, wide, mid, wide_mid) = refs[:8]
-    (slot_send, slot_recv, t_up, t_down, t_pair, t_recv, halo_send, halo_recv) = refs[8:16]
+    (slot_in, slots, held, lifted, total, ext, wide, mid, wide_mid) = refs[:9]
+    (slot_send, slot_recv, t_up, t_down, t_pair, t_recv, halo_send, halo_recv) = refs[9:17]
     if fused:
-        (own, whole, guest, normed, gate, up, hidden, kept, sent, came) = refs[16:26]
-        (recv, zup, zdown, side, core, pair) = refs[26:32]
-        sems = refs[32:37]
+        (own, whole, guest, normed, gate, up, hidden, kept, sent, came) = refs[17:27]
+        (recv, zup, zdown, side, core, pair) = refs[27:33]
+        sems = refs[33:38]
     cam, me = lax.axis_index("cam"), lax.axis_index("tile")
-    token_count = held.shape[2]
     barrier = pltpu.get_barrier_semaphore()
 
     def hello(other_cam, other_tile):
@@ -525,36 +521,22 @@
             ex, tokens, gain, guest, normed, gate, up, hidden, kept, sent, came, sems, send_slots
         )
         head_input = layer_norm(updated, head_gain[...]).astype(jnp.bfloat16)
-        scores = [
-            jnp.transpose(jnp.dot(head_input, weight[...], preferred_element_type=jnp.float32))
-            for weight in (w_depth, w_context)
-        ]
-        held[me] = soft_table(jnp.concatenate(scores, axis=0), bins)
+        logits = lax.dot_general(
+            w_depth[...], head_input, (((1,), (1,)), ((), ())), preferred_element_type=jnp.float32
+        )
+        context = jnp.dot(head_input, w_context[...], preferred_element_type=jnp.float32)
+        held[me] = table_of(soft_depth(logits), context)
     else:
         send_slots()
         held[me] = table_in[...]
-    tables = Tables(tiles, None, held, (t_up, t_down, t_pair), t_recv)
+    tables = Tables(tiles, held, (t_up, t_down, t_pair), t_recv)
     tables.begin()
     own_slots.wait()
     lax.fori_loop(1, tiles, slot_finish, 0)
-    splat(held, slots, total, bins, tables.sources(), tables.between)
-    channels = total.shape[1] // 2
-    per_scene = ROWS_DEV * GRID_W
-    for scene in range(SCN):
-        for row in range(ROWS_DEV):
-            start = scene * per_scene + row * GRID_W
-            side_of, first = divmod(start, total.shape[0])
-            ext[scene, 2 + row] = total[
-                first : first + GRID_W, side_of * channels : (side_of + 1) * channels
-            ].astype(jnp.bfloat16)
-
-    def halo(which):
-        if which == 0:
-            src, dst, other = ext.at[:, 2:4], ext.at[:, ROWS_DEV + 2 : ROWS_DEV + 4], me - 1
-        else:
-            src, dst, other = ext.at[:, ROWS_DEV : ROWS_DEV + 2], ext.at[:, 0:2], me + 1
-        return remote(src, dst, halo_send.at[which], halo_recv.at[which], cam, other)
-
+    total[...] = jnp.zeros_like(total)
+    channels = ext.shape[3]
+    rows_ext, rows_mid = ROWS_DEV + 4, ROWS_DEV + 2
+    has_before, has_after = me > 0, me + 1 < tiles
     blank = jnp.zeros((SCN, 2, GRID_W, channels), jnp.bfloat16)
 
     def first_tile():
@@ -563,22 +545,50 @@
     def last_tile():
         ext[:, ROWS_DEV + 2 : ROWS_DEV + 4] = blank
 
-    has_before, has_after = me > 0, me + 1 < tiles
-    pl.when(has_before)(lambda: halo(0).start())
-    pl.when(has_after)(lambda: halo(1).start())
     pl.when(me == 0)(first_tile)
     pl.when(me + 1 == tiles)(last_tile)
-    rows_ext = ROWS_DEV + 4
+
+    def halo(which, scene):
+        if which == 0:
+            src, dst, other = ext.at[scene, 2:4], ext.at[scene, ROWS_DEV + 2 : ROWS_DEV + 4], me - 1
+        else:
+            src, dst, other = ext.at[scene, ROWS_DEV : ROWS_DEV + 2], ext.at[scene, 0:2], me + 1
+        at = (which, scene)
+        return remote(src, dst, halo_send.at[at], halo_recv.at[at], cam, other)
+
+    def first_pass(turn, carry):
+        tables.between(turn)
+        source = tables.source(turn)
+        packed = slots[source]
+        value = lift(held.at[source], packed, token_count, bins)
+        lifted[source] = value.astype(jnp.bfloat16)
+        add_scene(total, 0, value, packed)
+        return carry
+
+    lax.fori_loop(0, tiles, first_pass, 0)
+    for scene in range(SCN):
+        if scene > 0:
+
+            def next_pass(source, carry):
+                add_scene(total, scene, lifted[source].astype(jnp.float32), slots[source])
+                return carry
+
+            lax.fori_loop(0, tiles, next_pass, 0)
+        for row in range(ROWS_DEV):
+            side_of, first = divmod(row * GRID_W, total.shape[1])
+            ext[scene, 2 + row] = total[
+                scene, first : first + GRID_W, side_of * channels : (side_of + 1) * channels
+            ].astype(jnp.bfloat16)
+        pl.when(has_before)(lambda: halo(0, scene).start())
+        pl.when(has_after)(lambda: halo(1, scene).start())
     for scene in range(SCN):
         for row in range(2, ROWS_DEV + 2):
             widen(ext, (scene, row), wide, scene * rows_ext + row)
-    pl.when(has_before)(lambda: halo(1).wait_recv())
-    pl.when(has_after)(lambda: halo(0).wait_recv())
     for scene in range(SCN):
+        pl.when(has_before)(lambda: halo(1, scene).wait_recv())
+        pl.when(has_after)(lambda: halo(0, scene).wait_recv())
         for row in (0, 1, ROWS_DEV + 2, ROWS_DEV + 3):
             widen(ext, (scene, row), wide, scene * rows_ext + row)
-    rows_mid = ROWS_DEV + 2
-    for scene in range(SCN):
         for row in range(rows_mid):
             value = jnp.maximum(convolve(wide, scene * rows_ext + row, w1) + b1[...], 0.0)
             if row == 0:
@@ -587,13 +597,13 @@
                 value = jnp.where(has_after, value, 0.0)
             mid[scene, row] = value.astype(jnp.bfloat16)
             widen(mid, (scene, row), wide_mid, scene * rows_mid + row)
-    for scene in range(SCN):
         for row in range(ROWS_DEV):
             value = convolve(wide_mid, scene * rows_mid + row, w2) + b2[...]
             value = ext[scene, 2 + row].astype(jnp.float32) + value
             out[scene, row] = value.astype(jnp.bfloat16)
-    pl.when(has_before)(lambda: halo(0).wait_send())
-    pl.when(has_after)(lambda: halo(1).wait_send())
+    for scene in range(SCN):
+        pl.when(has_before)(lambda: halo(0, scene).wait_send())
+        pl.when(has_after)(lambda: halo(1, scene).wait_send())
     tables.finish()
     if fused:
         finish()
@@ -605,12 +615,14 @@
     dma = pltpu.SemaphoreType.DMA
     bf16, f32 = jnp.bfloat16, jnp.float32
     slot_count = slots[0].shape[2]
-    slot_width = slot_count + -slot_count % CHUNK
+    slot_width = slot_count + -slot_count % LANES
+    table_rows = token_count + bins * pl.cdiv(token_count, LANES)
     scratch = [
         pltpu.VMEM((tiles, 1, slot_width), jnp.int32),
         pltpu.VMEM((tiles, 1, slot_width), jnp.int32),
-        pltpu.VMEM((tiles, bins + channels, token_count), bf16),
-        pltpu.VMEM((cells // 2, 2 * channels), f32),
+        pltpu.VMEM((tiles, table_rows, LANES), bf16),
+        pltpu.VMEM((tiles, channels, slot_width), bf16),
+        pltpu.VMEM((SCN, cells // SCN // 2, 2 * channels), f32),
         pltpu.VMEM((SCN, ROWS_DEV + 4, GRID_W, channels), bf16),
         pltpu.VMEM((SCN * (ROWS_DEV + 4), GRID_W, 3 * channels), bf16),
         pltpu.VMEM((SCN, ROWS_DEV + 2, GRID_W, channels), bf16),
@@ -621,8 +633,8 @@
         dma((tiles // 2,)),
         dma((tiles // 2,)),
         dma((tiles,)),
-        dma((2,)),
-        dma((2,)),
+        dma((2, SCN)),
+        dma((2, SCN)),
     ]
     operands = [*arrays, *slots, *weights]
     specs = [pl.BlockSpec(memory_space=pltpu.VMEM)] * len(operands)
@@ -658,7 +670,7 @@
             dma((pieces,)),
         ]
     return pl.pallas_call(
-        functools.partial(program, fused, tiles, bins),
+        functools.partial(program, fused, tiles, bins, token_count),
         out_shape=jax.ShapeDtypeStruct((SCN, ROWS_DEV, GRID_W, channels), bf16),
         in_specs=specs,
         out_specs=pl.BlockSpec(memory_space=pltpu.VMEM),
@@ -669,7 +681,7 @@
     )(*operands)
 
 
-def table_of(tokens, ln_gain, gate_weight, up_weight, down_weight, head_gain, head):
+def head_input_of(tokens, ln_gain, gate_weight, up_weight, down_weight, head_gain):
     inputs = tokens.astype(jnp.float32)
     normed = layer_norm(inputs, ln_gain).astype(jnp.bfloat16)
     axes = ("cam", "tile")
@@ -681,8 +693,7 @@
     down_whole = lax.all_gather(down_weight.T, axes, axis=0, tiled=True)
     contract = (((1,), (1,)), ((), ()))
     branch = lax.dot_general(hidden, down_whole, contract, preferred_element_type=jnp.float32)
-    head_input = layer_norm(inputs + branch, head_gain).astype(jnp.bfloat16)
-    return lax.dot_general(head, head_input, contract, preferred_element_type=jnp.float32)
+    return layer_norm(inputs + branch, head_gain).astype(jnp.bfloat16)
 
 
 def on_device(
@@ -716,19 +727,26 @@
     rows, units = gate_weight.shape
     fused = cams == 4 and tiles % 4 == 0 and rows % 16 == 0 and (rows * tiles) % LANES == 0
     if not fused:
-        head = jnp.concatenate([depth_weight, context_weight], axis=1).T
-        scores = table_of(
-            tokens, ln_gain, gate_weight, up_weight, down_weight, head_gain, head
-        )
-        return run(False, [soft_table(scores, bins)], slots, weights, sizes)
+        head_input = head_input_of(
+            tokens, ln_gain, gate_weight, up_weight, down_weight, head_gain
+        )
+        logits = lax.dot_general(
+            depth_weight,
+            head_input,
+            (((0,), (1,)), ((), ())),
+            preferred_element_type=jnp.float32,
+        )
+        context = jnp.dot(head_input, context_weight, preferred_element_type=jnp.float32)
+        table = table_of(soft_depth(logits), context)
+        return run(False, [table], slots, weights, sizes)
     arrays = [
         tokens,
         ln_gain.reshape(1, width),
         gate_weight,
         up_weight,
-        down_weight,
+        down_weight.T,
         head_gain.reshape(1, width),
-        depth_weight,
+        depth_weight.T,
         context_weight,
     ]
     return run(True, arrays, slots, weights, sizes)

time: 116 us -> 102 us (0.88)
  the two profiles are of different devices: /device:TPU:17 before, /device:TPU:0 now
where the time goes in v3:
time: 102 us
  Pallas kernels  100 us (98%)
  local copies, waits for them, and re-layouts  1.87 us (2%)
    pallas_call x1, Pallas kernels, run(): pl.pallas_call(functools.partial(program, fused, tiles, bins, token_count...  100 us

profile of v3, /device:TPU:0, one launch (start us, length us, event | category | flops | bytes accessed | tf_op | source)
XLA Modules:
  0.0 102.0 jit_solution(2895379640186584601)
XLA Ops:
  0.0 100.1 %shard_map.145 = bf16[2,4,256,128]{3,2,1,0:T(8,128)(2,1)} custom-call(bf16[176,1024]{1,0:T(8,128)(2,1)} %refs_0_.1, f32[1,1024]{1,0:T(1,128)} %bitcast.8, bf16[32,2730]{1,0:T(8,128)(2,1)} %refs_2_.1, bf16[32,2730]{1,0:T(8,128)(2,1)} %refs_3_.1, bf16[32,2730]{1,0:T(8,128)(2,1)} %bitcast.6, f32[1,1024]{1,0:T(1,128)} %bitcast.9, bf16[64,1024]{1,0:T(8,128)(2,1)} %bitcast.7, ...), custom_call_target="tpu_custom_call" | custom-call | tf_op jit(solution)/shard_map/pallas_call | solution.py:672
  100.2 1.9 %copy.17 = bf16[2,4,256,128]{3,2,1,0:T(8,128)(2,1)} copy(bf16[2,4,256,128]{3,2,1,0:T(8,128)(2,1)} %shard_map.145) | data formatting | bytes 1048576

commit v4 on v3

--- a/solution.py
+++ b/solution.py
@@ -255,7 +255,7 @@
             preferred_element_type=jnp.float32,
         )
         kept[piece] = got[:count]
-        sent[piece] = got[count:]
+        sent[piece] = got[count:].astype(jnp.bfloat16)
         part(piece).start()
 
     every = range(ex.depth)
@@ -289,7 +289,7 @@
         columns(2 * (1 - ex.y) + 1 - ex.c, near)
     for piece in range(kept.shape[0]):
         part(piece).wait_recv()
-    blocks = [kept[piece] + came[piece] for piece in range(kept.shape[0])]
+    blocks = [kept[piece] + came[piece].astype(jnp.float32) for piece in range(kept.shape[0])]
     updated = tokens[...].astype(jnp.float32) + jnp.concatenate(blocks, axis=1)
 
     def finish():
@@ -445,13 +445,19 @@
 
 
 def program(fused, tiles, bins, token_count, *refs):
+    count = 14 if fused else 7
+    operands, out, fetched, fetch = refs[:count], refs[count + 1], refs[-count:], refs[-count - 1]
+    live = refs[count]
+    refs = refs[count + 2 : -count - 1]
+    fetches = [
+        pltpu.make_async_copy(operand, place, fetch.at[i])
+        for i, (operand, place) in enumerate(zip(operands, fetched))
+    ]
+    (point, cell, w1, b1, w2, b2) = fetched[-6:]
     if fused:
-        (tokens, gain, w_gate, w_up, w_down, head_gain, w_depth, w_context) = refs[:8]
-        (point, cell, live, w1, b1, w2, b2, out) = refs[8:16]
-        refs = refs[16:]
+        (tokens, gain, w_gate, w_up, w_down, head_gain, w_depth, w_context) = fetched[:8]
     else:
-        (table_in, point, cell, live, w1, b1, w2, b2, out) = refs[:9]
-        refs = refs[9:]
+        table_in = fetched[0]
     (slot_in, slots, held, lifted, total, ext, wide, mid, wide_mid) = refs[:9]
     (slot_send, slot_recv, t_up, t_down, t_pair, t_recv, halo_send, halo_recv) = refs[9:17]
     if fused:
@@ -466,6 +472,9 @@
             barrier, inc=1, device_id={"cam": other_cam, "tile": other_tile}, device_id_type=MESH
         )
 
+    soon = (0, 1, 2, 3, 4, 8, 9) if fused else range(count)
+    for i in (*soon, *(i for i in range(count) if i not in soon)):
+        fetches[i].start()
     if fused:
         y, c = cam // 2, lax.rem(cam, 2)
         before, after = me >= 2, me + 2 < tiles
@@ -475,6 +484,8 @@
         pl.when(before)(lambda: hello(cam, me - 2))
         pl.when(after)(lambda: hello(cam, me + 2))
         expected = 3 + jnp.where(before, 1, 0) + jnp.where(after, 1, 0)
+        for i in soon:
+            fetches[i].wait()
         fill_own(w_gate, w_up, w_down, own)
         normed[:token_count] = layer_norm(tokens[...].astype(jnp.float32), gain[...]).astype(
             jnp.bfloat16
@@ -487,6 +498,8 @@
 
         lax.fori_loop(1, tiles, greet, 0)
         expected = tiles - 1
+        for i in soon:
+            fetches[i].wait()
     fill_slots(point, cell, live, slot_in, token_count * bins)
     pl.semaphore_wait(barrier, expected)
 
@@ -520,6 +533,9 @@
         updated, finish = feed_forward(
             ex, tokens, gain, guest, normed, gate, up, hidden, kept, sent, came, sems, send_slots
         )
+        for i in range(count):
+            if i not in soon:
+                fetches[i].wait()
         head_input = layer_norm(updated, head_gain[...]).astype(jnp.bfloat16)
         logits = lax.dot_general(
             w_depth[...], head_input, (((1,), (1,)), ((), ())), preferred_element_type=jnp.float32
@@ -556,6 +572,8 @@
         at = (which, scene)
         return remote(src, dst, halo_send.at[at], halo_recv.at[at], cam, other)
 
+    early = 3 * tiles // 8
+
     def first_pass(turn, carry):
         tables.between(turn)
         source = tables.source(turn)
@@ -563,17 +581,24 @@
         value = lift(held.at[source], packed, token_count, bins)
         lifted[source] = value.astype(jnp.bfloat16)
         add_scene(total, 0, value, packed)
+
+        def more_scenes():
+            for scene in range(1, SCN):
+                add_scene(total, scene, value, packed)
+
+        pl.when(turn < early)(more_scenes)
         return carry
 
     lax.fori_loop(0, tiles, first_pass, 0)
     for scene in range(SCN):
         if scene > 0:
 
-            def next_pass(source, carry):
+            def next_pass(turn, carry):
+                source = tables.source(turn)
                 add_scene(total, scene, lifted[source].astype(jnp.float32), slots[source])
                 return carry
 
-            lax.fori_loop(0, tiles, next_pass, 0)
+            lax.fori_loop(early, tiles, next_pass, 0)
         for row in range(ROWS_DEV):
             side_of, first = divmod(row * GRID_W, total.shape[1])
             ext[scene, 2 + row] = total[
@@ -636,9 +661,9 @@
         dma((2, SCN)),
         dma((2, SCN)),
     ]
-    operands = [*arrays, *slots, *weights]
-    specs = [pl.BlockSpec(memory_space=pltpu.VMEM)] * len(operands)
-    specs[len(arrays) + 2] = pl.BlockSpec(memory_space=pltpu.SMEM)
+    operands = [*arrays, *slots[:2], *weights]
+    specs = [pl.BlockSpec(memory_space=pl.ANY)] * len(operands)
+    specs += [pl.BlockSpec(memory_space=pltpu.SMEM)]
     if fused:
         tokens, gate_weight = arrays[0], arrays[2]
         count, width = tokens.shape
@@ -655,8 +680,8 @@
             pltpu.VMEM((2 * count, half), f32),
             pltpu.VMEM((2 * count, half), bf16),
             pltpu.VMEM((pieces, count, LANES), f32),
-            pltpu.VMEM((pieces, count, LANES), f32),
-            pltpu.VMEM((pieces, count, LANES), f32),
+            pltpu.VMEM((pieces, count, LANES), bf16),
+            pltpu.VMEM((pieces, count, LANES), bf16),
             dma((4, cams * tiles)),
             dma((4, 2, tiles)),
             dma((4, 2, tiles)),
@@ -669,6 +694,8 @@
             dma((pieces,)),
             dma((pieces,)),
         ]
+    scratch += [dma((len(operands),))]
+    scratch += [pltpu.VMEM(operand.shape, operand.dtype) for operand in operands]
     return pl.pallas_call(
         functools.partial(program, fused, tiles, bins, token_count),
         out_shape=jax.ShapeDtypeStruct((SCN, ROWS_DEV, GRID_W, channels), bf16),
@@ -678,7 +705,7 @@
         compiler_params=pltpu.CompilerParams(
             collective_id=0, has_side_effects=True, vmem_limit_bytes=60 * 1024 * 1024
         ),
-    )(*operands)
+    )(*operands, slots[2])
 
 
 def head_input_of(tokens, ln_gain, gate_weight, up_weight, down_weight, head_gain):

time: 102 us -> 96.7 us (0.948)
  Pallas kernels: 100 us -> 94.6 us
    pallas_call x1, Pallas kernels: 100 us -> 94.6 us  [run(): pl.pallas_call(functools.partial(program, fused, tiles, bins, token_count...]
where the time goes in v4:
time: 96.7 us; the launch traced here: 96.5 us
  Pallas kernels  94.6 us (98%)
  local copies, waits for them, and re-layouts  1.87 us (2%)
    pallas_call x1, Pallas kernels, run(): pl.pallas_call(functools.partial(program, fused, tiles, bins, token_count...  94.6 us

profile of v4, /device:TPU:0, one launch (start us, length us, event | category | flops | bytes accessed | tf_op | source)
XLA Modules:
  0.0 96.5 jit_solution(14256534313149215682)
XLA Ops:
  0.0 94.6 %shard_map.145 = bf16[2,4,256,128]{3,2,1,0:T(8,128)(2,1)} custom-call(bf16[176,1024]{1,0:T(8,128)(2,1)} %refs_0_.1, f32[1,1024]{1,0:T(1,128)} %bitcast.8, bf16[32,2730]{1,0:T(8,128)(2,1)} %refs_2_.1, bf16[32,2730]{1,0:T(8,128)(2,1)} %refs_3_.1, bf16[32,2730]{1,0:T(8,128)(2,1)} %bitcast.6, f32[1,1024]{1,0:T(1,128)} %bitcast.9, bf16[64,1024]{1,0:T(8,128)(2,1)} %bitcast.7, ...), custom_call_target="tpu_custom_call" | custom-call | tf_op jit(solution)/shard_map/pallas_call | solution.py:699
  94.6 1.9 %copy.17 = bf16[2,4,256,128]{3,2,1,0:T(8,128)(2,1)} copy(bf16[2,4,256,128]{3,2,1,0:T(8,128)(2,1)} %shard_map.145) | data formatting | bytes 1048576
